TPU v7x, 256 devices: a whole 4x4x8 slice. The times are simulated.
256 devices in a mesh: dp: 8 (over z_hi, x), expert: 32 (over y, z_lo, core).
Axes of the slice: x: 4, y: 4, z: 8 (z_hi: 2, z_lo: 4; z = z_hi * 4 + z_lo), core: 2. Of those that a mesh axis runs over, the one named last changes fastest.
Arguments:
- tokens: bfloat16 [40960, 2048], P(('dp', 'expert')), may hold values from -6 to 6
- out_grad: bfloat16 [40960, 2048], P(('dp', 'expert')), may hold values from -6 to 6
- expert_ids: int32 [40960, 8], P(('dp', 'expert')), may hold values from 0 to 127, all different within a row; in each aligned block of 160 rows (0 to 159, 160 to 319, ...) at most 15 rows name the same one
- gate_vals: bfloat16 [40960, 8], P(('dp', 'expert')), may hold values from 0.049804688 to 0.59765625
- w_gate: bfloat16 [32, 2048, 768], P('expert'), may hold values from -0.125 to 0.125
- w_up: bfloat16 [32, 2048, 768], P('expert'), may hold values from -0.125 to 0.125
- w_down: bfloat16 [32, 768, 2048], P('expert'), may hold values from -0.21875 to 0.21875
Outputs:
- d_tokens: bfloat16 [40960, 2048], P(('dp', 'expert'))
- d_gates: bfloat16 [40960, 8], P(('dp', 'expert'))
- d_w_gate: bfloat16 [32, 2048, 768], P('expert', 'dp')
- d_w_up: bfloat16 [32, 2048, 768], P('expert', 'dp')
- d_w_down: bfloat16 [32, 768, 2048], P('expert', None, 'dp')
Inputs may be any that keep to these rules, and one draw needn't show every extreme that they name: `expert_ids`: each row names 8 different experts and every expert is named somewhere. Among the 160 rows of one device no expert is named more than 15 times, a bound that some block reaches. Experts 32 and above lie outside this window.
All inputs are finite; a program needn't handle non-finite values.
Results may differ from a plain program's by a relative error of at most 0.012.
Values may be sent and summed in bfloat16 or wider, within the bound.
A program may use at most 128 MiB of HBM per device.

v0:
```python
import jax
import jax.numpy as jnp
from jax import lax
from jax.sharding import PartitionSpec as P

CAP = 15


def expert_rows(rows_x, rows_dy, rows_gate, gate_w, up_w, down_w):
    gate_pre = jnp.dot(rows_x, gate_w, preferred_element_type=jnp.float32)
    up_pre = jnp.dot(rows_x, up_w, preferred_element_type=jnp.float32)
    sigmoid_gate = jax.nn.sigmoid(gate_pre)
    silu_gate = gate_pre * sigmoid_gate
    hidden = (silu_gate * up_pre).astype(jnp.bfloat16)
    hidden_raw = lax.dot_general(
        rows_dy, down_w, (((1,), (1,)), ((), ())), preferred_element_type=jnp.float32
    )
    gate_scale = rows_gate.astype(jnp.float32)[:, None]
    gate_grad = jnp.sum(hidden.astype(jnp.float32) * hidden_raw, axis=1).astype(jnp.bfloat16)
    hidden_grad = gate_scale * hidden_raw
    up_grad = (hidden_grad * silu_gate).astype(jnp.bfloat16)
    pre_grad = (
        hidden_grad * up_pre * sigmoid_gate * (1.0 + gate_pre * (1.0 - sigmoid_gate))
    ).astype(jnp.bfloat16)
    scaled_dy = (gate_scale * rows_dy.astype(jnp.float32)).astype(jnp.bfloat16)
    input_rows = lax.dot_general(
        pre_grad, gate_w, (((1,), (1,)), ((), ())), preferred_element_type=jnp.float32
    )
    input_rows = input_rows + lax.dot_general(
        up_grad, up_w, (((1,), (1,)), ((), ())), preferred_element_type=jnp.float32
    )
    return (input_rows.astype(jnp.bfloat16), gate_grad, pre_grad, up_grad, hidden, scaled_dy)


def weight_grads(rows_x, scaled_dy, pre_grad, up_grad, hidden):
    hidden_units = hidden.shape[1]
    contract_rows = (((0,), (0,)), ((), ()))
    both_grads = jnp.concatenate([pre_grad, up_grad], axis=1)
    gate_up = lax.dot_general(rows_x, both_grads, contract_rows, preferred_element_type=jnp.float32)
    down_part = lax.dot_general(
        scaled_dy, hidden, contract_rows, preferred_element_type=jnp.float32
    )
    summed = lax.psum_scatter(
        jnp.concatenate([gate_up, down_part], axis=1).astype(jnp.bfloat16),
        "dp",
        scatter_dimension=0,
        tiled=True,
    ).astype(jnp.float32)
    return (
        summed[:, :hidden_units],
        summed[:, hidden_units : 2 * hidden_units],
        summed[:, 2 * hidden_units :].T,
    )


def body(tokens, out_grad, expert_ids, gate_vals, w_gate, w_up, w_down):
    expert_count = lax.axis_size("expert")
    tok_rows, features = tokens.shape
    top_count = expert_ids.shape[1]
    exp_local = w_gate.shape[0]
    experts = exp_local * expert_count
    pick_count = tok_rows * top_count
    slots_total = experts * CAP
    per_device = exp_local * CAP
    pick_expert = expert_ids.reshape(pick_count)
    inside = pick_expert < experts
    onehot = (pick_expert[:, None] == jnp.arange(experts, dtype=jnp.int32)[None, :]).astype(
        jnp.int32
    )
    before = jnp.cumsum(onehot, axis=0) - onehot
    pick_rank = jnp.sum(before * onehot, axis=1)
    pick_slot = jnp.where(inside, pick_expert * CAP + pick_rank, slots_total)
    slot_pick = (
        jnp.full((slots_total,), pick_count, jnp.int32)
        .at[pick_slot]
        .set(jnp.arange(pick_count, dtype=jnp.int32), mode="drop")
    )
    filled = slot_pick < pick_count
    safe_pick = jnp.minimum(slot_pick, pick_count - 1)
    slot_token = safe_pick // top_count
    send_x = jnp.where(
        filled[:, None], jnp.take(tokens, slot_token, axis=0), jnp.zeros((), tokens.dtype)
    )
    send_dy = jnp.where(
        filled[:, None], jnp.take(out_grad, slot_token, axis=0), jnp.zeros((), out_grad.dtype)
    )
    send_gate = jnp.where(
        filled, jnp.take(gate_vals.reshape(pick_count), safe_pick), jnp.zeros((), gate_vals.dtype)
    )
    recv_x, recv_dy, recv_gate = (
        lax.all_to_all(
            send_x.reshape(expert_count, per_device, features),
            "expert",
            split_axis=0,
            concat_axis=0,
            tiled=True,
        ),
        lax.all_to_all(
            send_dy.reshape(expert_count, per_device, features),
            "expert",
            split_axis=0,
            concat_axis=0,
            tiled=True,
        ),
        lax.all_to_all(
            send_gate.reshape(expert_count, per_device),
            "expert",
            split_axis=0,
            concat_axis=0,
            tiled=True,
        ),
    )
    recv_x = recv_x.reshape(expert_count, exp_local, CAP, features)
    recv_dy = recv_dy.reshape(expert_count, exp_local, CAP, features)
    recv_gate = recv_gate.reshape(expert_count, exp_local, CAP)
    rows_x = recv_x[:, 0].reshape(expert_count * CAP, features)
    rows_dy = recv_dy[:, 0].reshape(expert_count * CAP, features)
    rows_gate = recv_gate[:, 0].reshape(expert_count * CAP)
    input_rows, gate_grad, pre_grad, up_grad, hidden, scaled_dy = expert_rows(
        rows_x, rows_dy, rows_gate, w_gate[0], w_up[0], w_down[0]
    )
    back_rows = [input_rows.reshape(expert_count, CAP, features)]
    back_gates = [gate_grad.reshape(expert_count, CAP)]
    gate_sum, up_sum, down_sum = weight_grads(rows_x, scaled_dy, pre_grad, up_grad, hidden)
    grads_gate = [gate_sum.astype(jnp.bfloat16)]
    grads_up = [up_sum.astype(jnp.bfloat16)]
    grads_down = [down_sum.astype(jnp.bfloat16)]
    send_back = jnp.stack(back_rows, axis=1).reshape(expert_count, per_device, features)
    send_back_gate = jnp.stack(back_gates, axis=1).reshape(expert_count, per_device)
    back_x, back_gate = (
        lax.all_to_all(send_back, "expert", split_axis=0, concat_axis=0, tiled=True),
        lax.all_to_all(send_back_gate, "expert", split_axis=0, concat_axis=0, tiled=True),
    )
    flat_x = back_x.reshape(slots_total, features)
    flat_gate = back_gate.reshape(slots_total)
    safe_slot = jnp.minimum(pick_slot, slots_total - 1)
    pick_rows = jnp.where(
        inside[:, None], jnp.take(flat_x, safe_slot, axis=0).astype(jnp.float32), jnp.float32(0.0)
    )
    d_tokens = jnp.sum(pick_rows.reshape(tok_rows, top_count, features), axis=1).astype(
        jnp.bfloat16
    )
    d_gates = jnp.where(
        inside, jnp.take(flat_gate, safe_slot), jnp.zeros((), flat_gate.dtype)
    ).reshape(tok_rows, top_count)
    return (
        d_tokens,
        d_gates,
        jnp.stack(grads_gate, axis=0),
        jnp.stack(grads_up, axis=0),
        jnp.stack(grads_down, axis=0),
    )


def solution(mesh):
    in_specs = (
        P(("dp", "expert"), None),
        P(("dp", "expert"), None),
        P(("dp", "expert"), None),
        P(("dp", "expert"), None),
        P("expert", None, None),
        P("expert", None, None),
        P("expert", None, None),
    )
    out_specs = (
        P(("dp", "expert"), None),
        P(("dp", "expert"), None),
        P("expert", "dp", None),
        P("expert", "dp", None),
        P("expert", None, "dp"),
    )
    return jax.shard_map(body, mesh=mesh, in_specs=in_specs, out_specs=out_specs, check_vma=False)
```

profile of v0, /device:TPU:1, one launch (start us, length us, event | category | flops | bytes accessed | tf_op | source)
XLA Modules:
  0.0 434.9 jit_solution(1817945458205902199)
XLA Ops:
  9.9 15.9 %reduce-window.6 = s32[32,10,128]{2,1,0:T(8,128)S(1)} reduce-window(s32[32,10,128]{2,1,0:T(8,128)} %fusion.17, s32[]{:T(128)} %constant.56.clone.1), window={size=1x1x128 pad=0_0x0_0x127_0}, to_apply=%region_0.0 | reduce-window | flops 5201920 | bytes 327684 | tf_op jit(solution)/shard_map/reduce-window
  30.8 5.2 %scatter_custom_fusion = s32[480]{0:T(512)S(1)} fusion(s32[1280]{0:T(1024)S(1)} %get-tuple-element.22, s32[1280]{0:T(1024)S(1)} %iota.11, s32[]{:T(128)} %constant.59.clone.1), kind=kCustom, calls=%fused_computation.73 | custom fusion | bytes 1924 | tf_op jit(solution)/shard_map/scatter | solution.py:76
  36.1 3.5 gather_fusion
  40.3 10.2 %all-to-all-start = ((bf16[32,1,15]{2,1,0:T(2,128)(2,1)}), bf16[32,1,15]{2,1,0:T(2,128)(2,1)S(1)}, u32[]{:S(2)}, u32[]{:S(2)}) async-start(bf16[32,1,15]{2,1,0:T(2,128)(2,1)} %all_to_all.25), calls=%async_computation | async-start | bytes 32768 | tf_op jit(solution)/shard_map/all_to_all | solution.py:105
  50.5 6.4 %gather_fusion.3 = bf16[480,2048]{1,0:T(8,128)(2,1)} fusion(bf16[160,2048]{1,0:T(8,128)(2,1)} %param.10, s32[1024]{0:T(1024)S(1)} %pad_clamp_fusion.1), kind=kCustom, calls=%fused_computation.clone | custom fusion | bytes 3934080 | tf_op jit(solution)/shard_map/jit(_take)/gather | solution.py:85
  56.9 6.3 %gather_fusion.4 = bf16[480,2048]{1,0:T(8,128)(2,1)} fusion(bf16[160,2048]{1,0:T(8,128)(2,1)} %param.9, s32[1024]{0:T(1024)S(1)} %pad_clamp_fusion.1), kind=kCustom, calls=%fused_computation.1.clone | custom fusion | bytes 3934080 | tf_op jit(solution)/shard_map/jit(_take)/gather | solution.py:82
  63.3 4.6 %select_select_fusion.1 = (bf16[480,2048]{1,0:T(8,128)(2,1)}, bf16[480,2048]{1,0:T(8,128)(2,1)}) fusion(bf16[480,2048]{1,0:T(8,128)(2,1)} %gather_fusion.3, pred[480]{0:T(512)(128)(4,1)S(1)} %get-tuple-element.29, pred[480]{0:T(512)(128)(4,1)S(1)} %get-tuple-element.28, bf16[480,2048]{1,0:T(8,128)(2,1)} %gather_fusion.4), kind=kLoop, calls=%fused_computation.24 | loop fusion | flops 3932160 | bytes 7865280 | tf_op jit(solution)/shard_map/jit(_where)/select_n | solution.py:84
  70.7 7.7 %all-to-all-start.2 = ((bf16[32,15,2048]{2,1,0:T(8,128)(2,1)}), bf16[32,15,2048]{2,1,0:T(8,128)(2,1)}, u32[]{:S(2)}, u32[]{:S(2)}) async-start(bf16[32,15,2048]{2,1,0:T(8,128)(2,1)} %reshape.176), calls=%async_computation.2 | async-start | bytes 4194304 | tf_op jit(solution)/shard_map/all_to_all | solution.py:91
  81.3 47.0 %all-to-all-done.2 = bf16[32,15,2048]{2,1,0:T(8,128)(2,1)} async-done(((bf16[32,15,2048]{2,1,0:T(8,128)(2,1)}), bf16[32,15,2048]{2,1,0:T(8,128)(2,1)}, u32[]{:S(2)}, u32[]{:S(2)}) %all-to-all-start.2) | async-done | bytes 1966112 | tf_op jit(solution)/shard_map/all_to_all | solution.py:91
  128.4 5.1 %all-to-all-start.1 = ((bf16[32,15,2048]{2,1,0:T(8,128)(2,1)}), bf16[32,15,2048]{2,1,0:T(8,128)(2,1)}, u32[]{:S(2)}, u32[]{:S(2)}) async-start(bf16[32,15,2048]{2,1,0:T(8,128)(2,1)} %reshape.175), calls=%async_computation.1 | async-start | bytes 4194304 | tf_op jit(solution)/shard_map/all_to_all | solution.py:98
  136.8 5.4 %fusion.6 = f32[480,768]{1,0:T(8,128)} fusion(bf16[480,2048]{1,0:T(8,128)(2,1)} %reshape_squeeze_reshape.8, bf16[1,2048,768]{2,1,0:T(8,128)(2,1)} %param.14), kind=kOutput, calls=%fused_computation.19 | convolution fusion | flops 1509949440 | bytes 6586368 | tf_op jit(solution)/shard_map/dot_general | solution.py:11
  145.1 38.4 %all-to-all-done.1 = bf16[32,15,2048]{2,1,0:T(8,128)(2,1)} async-done(((bf16[32,15,2048]{2,1,0:T(8,128)(2,1)}), bf16[32,15,2048]{2,1,0:T(8,128)(2,1)}, u32[]{:S(2)}, u32[]{:S(2)}) %all-to-all-start.1) | async-done | bytes 1966112 | tf_op jit(solution)/shard_map/all_to_all | solution.py:98
  186.4 5.9 %multiply_reduce_fusion = (bf16[480]{0:T(512)(128)(2,1)S(1)}, bf16[480,768]{1,0:T(8,128)(2,1)S(1)}, bf16[480,768]{1,0:T(8,128)(2,1)S(1)}, bf16[480,768]{1,0:T(8,128)(2,1)S(1)}) fusion(f32[480,768]{1,0:T(8,128)} %fusion.6, f32[480,768]{1,0:T(8,128)} %fusion.2, f32[480]{0:T(512)S(1)} %reshape.179, bf16[480,2048]{1,0:T(8,128)(2,1)} %reshape_squeeze_reshape.7, ...), kind=kOutput, calls=%fused_computation.29 | convolution fusion | flops 1516953088 | bytes 10275648 | tf_op jit(solution)/shard_map/dot_general | solution.py:15
  194.4 3.8 convolution_convert_fusion
  198.2 11.4 %pad_maximum_fusion = bf16[2048,2304]{0,1:T(8,128)(2,1)} fusion(bf16[2048,768]{0,1:T(8,128)(2,1)S(1)} %convolution_convert_fusion.1, bf16[2048,1536]{0,1:T(8,128)(2,1)S(1)} %convolution_convert_fusion), kind=kLoop, calls=%fused_computation.7 | loop fusion | flops 18874368 | bytes 18874368 | tf_op jit(solution)/shard_map/concatenate | solution.py:44
  210.3 4.4 %all-to-all-start.4 = ((bf16[32,1,15]{2,1,0:T(2,128)(2,1)}), bf16[32,1,15]{2,1,0:T(2,128)(2,1)S(1)}, u32[]{:S(2)}, u32[]{:S(2)}) async-start(bf16[32,1,15]{2,1,0:T(2,128)(2,1)} %convert_element_type.84), calls=%async_computation.4 | async-start | bytes 32768 | tf_op jit(solution)/shard_map/all_to_all | solution.py:132
  214.8 3.0 fusion
  220.8 3.1 reshape_stack_reshape.4
  223.9 7.7 %all-to-all-start.3 = ((bf16[32,15,2048]{2,1,0:T(8,128)(2,1)}), bf16[32,15,2048]{2,1,0:T(8,128)(2,1)}, u32[]{:S(2)}, u32[]{:S(2)}) async-start(bf16[32,15,2048]{2,1,0:T(8,128)(2,1)} %reshape_stack_reshape.4), calls=%async_computation.3 | async-start | bytes 4194304 | tf_op jit(solution)/shard_map/all_to_all | solution.py:131
  231.9 8.0 %gather_fusion.2 = bf16[1280]{0:T(1024)(128)(2,1)S(1)} fusion(bf16[480]{0:T(512)(128)(2,1)S(1)} %reshape.178, s32[2048]{0:T(1024)S(1)} %pad_clamp_fusion), kind=kCustom, calls=%fused_computation.4 | custom fusion | bytes 10240 | tf_op jit(solution)/shard_map/jit(_take)/gather | solution.py:144
  240.7 130.8 %all-to-all-done.3 = bf16[32,15,2048]{2,1,0:T(8,128)(2,1)} async-done(((bf16[32,15,2048]{2,1,0:T(8,128)(2,1)}), bf16[32,15,2048]{2,1,0:T(8,128)(2,1)}, u32[]{:S(2)}, u32[]{:S(2)}) %all-to-all-start.3) | async-done | bytes 1966112 | tf_op jit(solution)/shard_map/all_to_all | solution.py:131
  374.4 12.6 %gather_fusion.1 = bf16[1280,2048]{1,0:T(8,128)(2,1)} fusion(bf16[480,2048]{1,0:T(8,128)(2,1)} %reshape.177, s32[2048]{0:T(1024)S(1)} %pad_clamp_fusion), kind=kCustom, calls=%fused_computation.3 | custom fusion | bytes 10490880 | tf_op jit(solution)/shard_map/jit(_take)/gather | solution.py:138
  387.0 6.5 %select_reduce_fusion = bf16[160,2048]{1,0:T(8,128)(2,1)} fusion(bf16[1280,2048]{1,0:T(8,128)(2,1)} %gather_fusion.1, pred[160,8]{1,0:T(8,128)(4,1)S(1)} %get-tuple-element.24, pred[160,8]{1,0:T(8,128)(4,1)S(1)} %broadcast_compare_fusion), kind=kLoop, calls=%fused_computation.6 | loop fusion | flops 10158080 | bytes 5900800 | tf_op jit(solution)/shard_map/reduce_sum | solution.py:140
  393.5 29.5 %reduce-scatter.2.cloned.1.call-done = bf16[256,2304]{0,1:T(8,128)(2,1)} async-done(((bf16[2048,2304]{0,1:T(8,128)(2,1)}), bf16[256,2304]{0,1:T(8,128)(2,1)}) %reduce-scatter.2.cloned.1.call-update) | async-done | bytes 1179664 | tf_op jit(solution)/shard_map/reduce_scatter | solution.py:43
  (67 shorter events, 37.8 us)
Async XLA Ops:
  7.2 135.1 %copy-start = (bf16[1,2048,768]{2,1,0:T(8,128)(2,1)S(1)}, bf16[1,2048,768]{2,1,0:T(8,128)(2,1)}, u32[]{:S(2)}) copy-start(bf16[1,2048,768]{2,1,0:T(8,128)(2,1)} %param.13) | copy-start | bytes 9437188
  7.2 21.6 %copy-start.4 = (bf16[160,8]{0,1:T(8,128)(2,1)S(1)}, bf16[160,8]{0,1:T(8,128)(2,1)}, u32[]{:S(2)}) copy-start(bf16[160,8]{0,1:T(8,128)(2,1)} %param.12) | copy-start | bytes 7684
  40.3 30.4 %all-to-all-start = ((bf16[32,1,15]{2,1,0:T(2,128)(2,1)}), bf16[32,1,15]{2,1,0:T(2,128)(2,1)S(1)}, u32[]{:S(2)}, u32[]{:S(2)}) async-start(bf16[32,1,15]{2,1,0:T(2,128)(2,1)} %all_to_all.25), calls=%async_computation | async-start | bytes 32768 | tf_op jit(solution)/shard_map/all_to_all | solution.py:105
  70.7 57.7 %all-to-all-start.2 = ((bf16[32,15,2048]{2,1,0:T(8,128)(2,1)}), bf16[32,15,2048]{2,1,0:T(8,128)(2,1)}, u32[]{:S(2)}, u32[]{:S(2)}) async-start(bf16[32,15,2048]{2,1,0:T(8,128)(2,1)} %reshape.176), calls=%async_computation.2 | async-start | bytes 4194304 | tf_op jit(solution)/shard_map/all_to_all | solution.py:91
  128.4 55.2 %all-to-all-start.1 = ((bf16[32,15,2048]{2,1,0:T(8,128)(2,1)}), bf16[32,15,2048]{2,1,0:T(8,128)(2,1)}, u32[]{:S(2)}, u32[]{:S(2)}) async-start(bf16[32,15,2048]{2,1,0:T(8,128)(2,1)} %reshape.175), calls=%async_computation.1 | async-start | bytes 4194304 | tf_op jit(solution)/shard_map/all_to_all | solution.py:98
  133.5 289.5 %reduce-scatter.2.cloned.1.call-start = ((), (), s32[]{:S(2)}) async-start(), calls=%async_computation.6 | async-start | bytes 10616832 | tf_op jit(solution)/shard_map/reduce_scatter | solution.py:43
  136.8 5.5 %copy-start.1 = (bf16[480,2048]{1,0:T(8,128)(2,1)S(1)}, bf16[480,2048]{1,0:T(8,128)(2,1)}, u32[]{:S(2)}) copy-start(bf16[480,2048]{1,0:T(8,128)(2,1)} %reshape_squeeze_reshape.8) | copy-start | bytes 5898244
  186.4 5.9 %copy-start.3 = (bf16[480,2048]{1,0:T(8,128)(2,1)S(1)}, bf16[480,2048]{1,0:T(8,128)(2,1)}, u32[]{:S(2)}) copy-start(bf16[480,2048]{1,0:T(8,128)(2,1)} %reshape_squeeze_reshape.7) | copy-start | bytes 5898244
  192.3 2.0 copy-start.6
  192.3 2.0 copy-start.7
  192.3 2.1 copy-start.2
  210.3 13.6 %all-to-all-start.4 = ((bf16[32,1,15]{2,1,0:T(2,128)(2,1)}), bf16[32,1,15]{2,1,0:T(2,128)(2,1)S(1)}, u32[]{:S(2)}, u32[]{:S(2)}) async-start(bf16[32,1,15]{2,1,0:T(2,128)(2,1)} %convert_element_type.84), calls=%async_computation.4 | async-start | bytes 32768 | tf_op jit(solution)/shard_map/all_to_all | solution.py:132
  214.7 3.0 copy-start.5
  214.7 3.0 copy-start.8
  223.9 147.6 %all-to-all-start.3 = ((bf16[32,15,2048]{2,1,0:T(8,128)(2,1)}), bf16[32,15,2048]{2,1,0:T(8,128)(2,1)}, u32[]{:S(2)}, u32[]{:S(2)}) async-start(bf16[32,15,2048]{2,1,0:T(8,128)(2,1)} %reshape_stack_reshape.4), calls=%async_computation.3 | async-start | bytes 4194304 | tf_op jit(solution)/shard_map/all_to_all | solution.py:131
Sparse Core Ops, SparseCore 0:
  209.7 213.2 reduce-scatter.1
where the time goes:
time: 437 us; the launch traced here: 435 us
  waiting for transfers between devices  246 us (56%)
  local copies, waits for them, and re-layouts  71.3 us (16%)
  other arithmetic  42 us (10%)
  starting transfers between devices  35.4 us (8%)
  matrix products  25.9 us (6%)
  between operations  14.4 us (3%)
    all_to_all x1, waiting for transfers between devices, body(): lax.all_to_all(send_back, 'expert', split_axis=0, concat_axis=0, tiled=True)  131 us
    all_to_all x1, waiting for transfers between devices, body(): lax.all_to_all(send_x.reshape(expert_count, per_device, features), 'exper...  47 us
    all_to_all x1, waiting for transfers between devices, body(): lax.all_to_all(send_dy.reshape(expert_count, per_device, features), 'expe...  38.4 us
    reduce_scatter x1, waiting for transfers between devices, weight_grads(): lax.psum_scatter(jnp.concatenate([gate_up, down_part], axis=1).astype(jnp...  29.5 us
    another operation x3, other arithmetic  16.8 us
    gather x1, local copies, waits for them, and re-layouts, body(): jnp.take(flat_x, safe_slot, axis=0).astype(jnp.float32)  12.6 us
    concatenate x1, other arithmetic, weight_grads(): jnp.concatenate([gate_up, down_part], axis=1).astype(jnp.bfloat16)  11.4 us
    all_to_all x1, starting transfers between devices, body(): lax.all_to_all(send_gate.reshape(expert_count, per_device), 'expert', spl...  10.2 us
  transfers between devices with their start and end apart: 6, of which 4 were waited for; matrix products, arithmetic and copies ran while one was open for 17% of the time, Pallas kernels for 0%

commit v1 on v0

v1 whole, which is shorter than its diff:
```python
import functools

import jax
import jax.numpy as jnp
from jax import lax
from jax.experimental import pallas as pl
from jax.experimental.pallas import tpu as pltpu
from jax.sharding import PartitionSpec as P

MESH = pl.DeviceIdType.MESH
BF = jnp.bfloat16
F32 = jnp.float32

TOK = 160
TOP = 8
D = 2048
FF = 768
NE = 32
SLOT = 16
ROWS = NE * SLOT
GL = NE * SLOT
UNITS = 6
MSGS = 6
HALF = 128


def coords():
    dp, ex = lax.axis_index("dp"), lax.axis_index("expert")
    return dp % 4, ex // 8, (dp // 4) * 4 + (ex // 2) % 4, ex % 2


def device(x, y, z, c):
    z = (z + 8) % 8
    return {"dp": (z // 4) * 4 + (x + 4) % 4, "expert": (((y + 4) % 4) * 4 + z % 4) * 2 + c}


def offset(j):
    i = (j // 2) % 4
    return i, (i + j // 8) % 4, j % 2


def z_shift(kind, core):
    return jnp.where(kind == 1, 1, 0) - jnp.where(kind == 2, 1, 0) + jnp.where(kind == 3, 2 - 4 * core, 0)


def target(j):
    x, y, z, c = coords()
    dy, kind, dc = offset(j)
    return device(x, y + dy, z + z_shift(kind, c), (c + dc) % 2)


def origin(j):
    x, y, z, c = coords()
    dy, kind, dc = offset(j)
    c0 = (c + dc) % 2
    return device(x, y - dy, z - z_shift(kind, c0), c0)


def target_expert(j):
    x, y, z, c = coords()
    dy, kind, dc = offset(j)
    return (((y + dy) % 4) * 4 + (z + z_shift(kind, c) + 8) % 4) * 2 + (c + dc) % 2


def peers():
    x, y, z, c = coords()
    for dz in (0, 1, -1, 2, -2):
        for dy in range(4):
            for dc in (0, 1):
                if (dz, dy, dc) != (0, 0, 0):
                    yield device(x, y + dy, z + dz, (c + dc) % 2)
    yield device(x + 1, y, z, c)
    yield device(x - 1, y, z, c)
    yield device(x, y, z + 4, c)


def block(j):
    return pl.ds(pl.multiple_of(j * SLOT, SLOT), SLOT)


def iota(shape, dim):
    return lax.broadcasted_iota(jnp.int32, shape, dim)


def kernel(
    ids_ref, gate_ref, tok_ref, dy_ref, wg_hbm, wu_hbm, wd_hbm,
    dtok_ref, dgate_ref, owg_ref, owu_ref, owd_ref,
    wg, wu, wd, sent, xs, sel, gs, rt, back, dgs, rs_s, rs_r, own, z_s, z_r,
    w_sem, d_ss, d_rs, b_ss, b_rs, r_ss, r_rs, z_ss, z_rs,
):
    x, y, z, c = coords()
    me = lax.axis_index("expert")
    my_half = lax.axis_index("dp") // 4

    barrier = pltpu.get_barrier_semaphore()
    count = 0
    for peer in peers():
        pl.semaphore_signal(barrier, inc=1, device_id=peer, device_id_type=MESH)
        count += 1

    loads = [
        pltpu.make_async_copy(src.at[0], dst, w_sem.at[n])
        for n, (src, dst) in enumerate(((wg_hbm, wg), (wu_hbm, wu), (wd_hbm, wd)))
    ]
    for load in loads:
        load.start()

    expert_of = iota((TOK, GL), 1) // SLOT
    member = jnp.zeros((TOK, GL), F32)
    value = jnp.zeros((TOK, GL), F32)
    for k in range(TOP):
        hit = ids_ref[:, k : k + 1] == expert_of
        member = jnp.where(hit, 1.0, member)
        value = jnp.where(hit, gate_ref[:, k : k + 1].astype(F32), value)
    earlier = (iota((TOK, TOK), 1) < iota((TOK, TOK), 0)).astype(F32).astype(BF)
    rank = jnp.dot(earlier, member.astype(BF), preferred_element_type=F32)
    slot_of = (iota((TOK, GL), 1) % SLOT).astype(F32)
    chosen = jnp.where(rank == slot_of, member, 0.0)
    sel[...] = chosen.astype(BF)
    gate_row = jnp.sum(chosen * value, axis=0, keepdims=True)
    pick = chosen.T.astype(BF)
    last = iota((ROWS, 512), 0) % SLOT == SLOT - 1
    for p, ref in enumerate((tok_ref, dy_ref)):
        for n in range(D // 512):
            cols = pl.ds(n * 512, 512)
            rows = jnp.dot(pick, ref[:, cols], preferred_element_type=F32)
            if p == 0 and n == 0:
                rows = jnp.where(last, gate_row, rows)
            sent[p, :, cols] = rows.astype(BF)

    pl.semaphore_wait(barrier, count)

    def dispatch(p, j):
        return pltpu.make_async_remote_copy(
            src_ref=sent.at[p, block(target_expert(j))],
            dst_ref=xs.at[p, block(j)],
            send_sem=d_ss.at[p, j],
            recv_sem=d_rs.at[p, j],
            device_id=target(j),
            device_id_type=MESH,
        )

    @pl.loop(1, NE)
    def _(j):
        dispatch(0, j).start()
        dispatch(1, j).start()

    for p in range(2):
        xs[p, 0:SLOT, :] = sent[p, block(me), :]
    for load in loads:
        load.wait()

    @pl.loop(1, NE)
    def _(j):
        dispatch(0, j).wait_recv()
        dispatch(1, j).wait_recv()

    lane = iota((1, SLOT, GL), 2)
    mine = lane == me * SLOT + iota((1, SLOT, GL), 1)

    def expert(rows, count):
        row = xs[0, rows, 0:GL].astype(F32).reshape(count // SLOT, SLOT, GL)
        row = jnp.where(iota((1, SLOT, GL), 1) == SLOT - 1, row, 0.0)
        row = jnp.sum(row, axis=1, keepdims=True)
        scale = jnp.sum(jnp.where(mine, row, 0.0), axis=2, keepdims=True).reshape(count, 1)

        def part(f, total):
            cols = pl.ds(pl.multiple_of(f * 256, 256), 256)
            gate_pre = jnp.dot(xs[0, rows, :], wg[:, cols], preferred_element_type=F32)
            up_pre = jnp.dot(xs[0, rows, :], wu[:, cols], preferred_element_type=F32)
            raw = lax.dot_general(
                xs[1, rows, :], wd[cols, :], (((1,), (1,)), ((), ())), preferred_element_type=F32
            )
            sig = jax.nn.sigmoid(gate_pre)
            silu = gate_pre * sig
            hidden = (silu * up_pre).astype(BF)
            grad = scale * raw
            gs[2, rows, cols] = (grad * silu).astype(BF)
            gs[1, rows, cols] = (grad * up_pre * sig * (1.0 + gate_pre * (1.0 - sig))).astype(BF)
            gs[0, rows, cols] = hidden
            return total + jnp.sum(hidden.astype(F32) * raw, axis=1, keepdims=True)

        total = lax.fori_loop(0, FF // 256, part, jnp.zeros((count, 1), F32))
        grads = total.astype(BF).astype(F32).reshape(count // SLOT, SLOT, 1)
        grads = jnp.sum(jnp.where(mine, grads, 0.0), axis=1, keepdims=True)
        grads = jnp.broadcast_to(grads, (count // SLOT, SLOT, GL)).reshape(count, GL)
        dgs[rows, :] = grads.astype(BF)
        xs[1, rows, :] = (scale * xs[1, rows, :].astype(F32)).astype(BF)

    @pl.loop(0, 2)
    def _(m):
        expert(pl.ds(pl.multiple_of(m * 256, 256), 256), 256)

    def half_of(u):
        return jnp.where(u < 3, 1 - my_half, my_half)

    def tile(u, to_x, half):
        kind = u % 3
        start = (half_of(u) * 4 + (to_x + 4) % 4) * 256 + half * HALF
        left = xs[jnp.where(kind == 0, 1, 0), :, pl.ds(pl.multiple_of(start, HALF), HALF)]
        return lax.dot_general(
            left, gs[kind], (((0,), (0,)), ((), ())), preferred_element_type=F32
        )

    def message(u, m):
        step = 1 if m % 2 == 0 else -1
        return pltpu.make_async_remote_copy(
            src_ref=rs_s.at[u * MSGS + m],
            dst_ref=rs_r.at[u * MSGS + m],
            send_sem=r_ss.at[u * MSGS + m],
            recv_sem=r_rs.at[u * MSGS + m],
            device_id=device(x + step, y, z, c),
            device_id_type=MESH,
        )

    def send(u, m, tile_value):
        rs_s[u * MSGS + m] = tile_value.astype(BF)
        message(u, m).start()

    def received(u, m):
        message(u, m).wait_recv()
        return rs_r[u * MSGS + m].astype(F32)

    def to_partner(n, half):
        return pltpu.make_async_remote_copy(
            src_ref=z_s.at[n * 2 + half],
            dst_ref=z_r.at[n * 2 + half],
            send_sem=z_ss.at[n * 2 + half],
            recv_sem=z_rs.at[n * 2 + half],
            device_id=device(x, y, z + 4, c),
            device_id_type=MESH,
        )

    def give_back(j):
        return pltpu.make_async_remote_copy(
            src_ref=rt.at[block(j)],
            dst_ref=back.at[block(me)],
            send_sem=b_ss.at[j],
            recv_sem=b_rs.at[j],
            device_id=origin(j),
            device_id_type=MESH,
        )

    def returns():
        ends = iota((ROWS, 512), 0) % SLOT == SLOT - 1

        @pl.loop(0, D // 512)
        def _(n):
            feats = pl.ds(pl.multiple_of(n * 512, 512), 512)
            contract = (((1,), (1,)), ((), ()))
            rows = lax.dot_general(gs[1], wg[feats, :], contract, preferred_element_type=F32)
            rows = rows + lax.dot_general(gs[2], wu[feats, :], contract, preferred_element_type=F32)
            rt[:, feats] = rows.astype(BF)

        rt[:, 0:GL] = jnp.where(ends, dgs[...].astype(F32), rt[:, 0:GL].astype(F32)).astype(BF)

        @pl.loop(1, NE)
        def _(j):
            give_back(j).start()

        back[block(me), :] = rt[0:SLOT, :]

    @pl.loop(0, UNITS + 2)
    def _(v):
        @pl.when(v < UNITS)
        def _():
            u = v
            send(u, 0, tile(u, x + 2, 0))
            send(u, 1, tile(u, x + 2, 1))
            send(u, 2, tile(u, x + 1, 1))
            send(u, 3, tile(u, x - 1, 0))

        @pl.when(v == 1)
        def _():
            returns()

        @pl.when((v >= 1) & (v < UNITS + 1))
        def _():
            u = v - 1
            send(u, 4, tile(u, x + 1, 0) + received(u, 0))
            send(u, 5, tile(u, x - 1, 1) + received(u, 1))

        @pl.when(v >= 2)
        def _():
            u = v - 2
            for half in range(2):
                total = tile(u, x, half) + received(u, 4 + half) + received(u, 3 - half)

                @pl.when(u < 3)
                def _():
                    z_s[u * 2 + half] = total.astype(BF)
                    to_partner(u, half).start()

                @pl.when(u >= 3)
                def _():
                    own[(u - 3) * 2 + half] = total

    @pl.loop(1, NE)
    def _(j):
        give_back(j).wait_recv()

    for n in range(D // 512):
        cols = pl.ds(n * 512, 512)
        dtok_ref[:, cols] = jnp.dot(sel[...], back[:, cols], preferred_element_type=F32).astype(BF)
    ends = iota((ROWS, GL), 0) % SLOT == SLOT - 1
    row = jnp.sum(jnp.where(ends, back[:, 0:GL].astype(F32), 0.0), axis=0, keepdims=True)
    picked = sel[...].astype(F32) * row
    at = iota((TOK, TOP), 1)
    grads = jnp.zeros((TOK, TOP), F32)
    for k in range(TOP):
        hit = ids_ref[:, k : k + 1] == expert_of
        one = jnp.sum(jnp.where(hit, picked, 0.0), axis=1, keepdims=True)
        grads = jnp.where(at == k, one, grads)
    dgate_ref[...] = grads.astype(BF)

    for n, ref in enumerate((owd_ref, owg_ref, owu_ref)):
        for half in range(2):
            to_partner(n, half).wait_recv()
            total = own[n * 2 + half] + z_r[n * 2 + half].astype(F32)
            if n == 0:
                ref[0, :, half * HALF : (half + 1) * HALF] = total.T.astype(BF)
            else:
                ref[0, half * HALF : (half + 1) * HALF, :] = total.astype(BF)

    @pl.loop(1, NE)
    def _(j):
        dispatch(0, j).wait_send()
        dispatch(1, j).wait_send()
        give_back(j).wait_send()

    @pl.loop(0, UNITS)
    def _(u):
        for m in range(MSGS):
            message(u, m).wait_send()

    for n in range(3):
        for half in range(2):
            to_partner(n, half).wait_send()


def body(tokens, out_grad, expert_ids, gate_vals, w_gate, w_up, w_down):
    vmem = pl.BlockSpec(memory_space=pltpu.VMEM)
    hbm = pl.BlockSpec(memory_space=pl.ANY)
    dma = pltpu.SemaphoreType.DMA
    return pl.pallas_call(
        kernel,
        out_shape=(
            jax.ShapeDtypeStruct((TOK, D), BF),
            jax.ShapeDtypeStruct((TOK, TOP), BF),
            jax.ShapeDtypeStruct((1, 256, FF), BF),
            jax.ShapeDtypeStruct((1, 256, FF), BF),
            jax.ShapeDtypeStruct((1, FF, 256), BF),
        ),
        in_specs=[vmem] * 4 + [hbm] * 3,
        out_specs=[vmem] * 5,
        scratch_shapes=[
            pltpu.VMEM((D, FF), BF),
            pltpu.VMEM((D, FF), BF),
            pltpu.VMEM((FF, D), BF),
            pltpu.VMEM((2, ROWS, D), BF),
            pltpu.VMEM((2, ROWS, D), BF),
            pltpu.VMEM((TOK, GL), BF),
            pltpu.VMEM((3, ROWS, FF), BF),
            pltpu.VMEM((ROWS, D), BF),
            pltpu.VMEM((ROWS, D), BF),
            pltpu.VMEM((ROWS, GL), BF),
            pltpu.VMEM((UNITS * MSGS, HALF, FF), BF),
            pltpu.VMEM((UNITS * MSGS, HALF, FF), BF),
            pltpu.VMEM((6, HALF, FF), F32),
            pltpu.VMEM((6, HALF, FF), BF),
            pltpu.VMEM((6, HALF, FF), BF),
            dma((3,)),
            dma((2, NE)),
            dma((2, NE)),
            dma((NE,)),
            dma((NE,)),
            dma((UNITS * MSGS,)),
            dma((UNITS * MSGS,)),
            dma((6,)),
            dma((6,)),
        ],
        compiler_params=pltpu.CompilerParams(
            collective_id=0, has_side_effects=True, vmem_limit_bytes=60 * 2**20
        ),
    )(expert_ids, gate_vals, tokens, out_grad, w_gate, w_up, w_down)


def solution(mesh):
    in_specs = (
        P(("dp", "expert"), None),
        P(("dp", "expert"), None),
        P(("dp", "expert"), None),
        P(("dp", "expert"), None),
        P("expert", None, None),
        P("expert", None, None),
        P("expert", None, None),
    )
    out_specs = (
        P(("dp", "expert"), None),
        P(("dp", "expert"), None),
        P("expert", "dp", None),
        P("expert", "dp", None),
        P("expert", None, "dp"),
    )
    return jax.shard_map(body, mesh=mesh, in_specs=in_specs, out_specs=out_specs, check_vma=False)
```

time: 437 us -> 174 us (0.40)
  the two profiles are of different devices: /device:TPU:1 before, /device:TPU:69 now
where the time goes in v1:
time: 174 us
  Pallas kernels  163 us (94%)
  local copies, waits for them, and re-layouts  10.6 us (6%)
    pallas_call x1, Pallas kernels, body(): pl.pallas_call(kernel, out_shape=(jax.ShapeDtypeStruct((TOK, D), BF), jax...  163 us
    unnamed x8, local copies, waits for them, and re-layouts  9.12 us

profile of v1, /device:TPU:69, one launch (start us, length us, event | category | flops | bytes accessed | tf_op | source)
XLA Modules:
  0.0 173.8 jit_solution(3762990484133968915)
XLA Ops:
  0.6 1.4 copy.13.gate_ref
  2.0 1.4 copy.12.ids_ref
  3.5 162.6 %shard_map.110 = (bf16[160,2048]{1,0:T(8,128)(2,1)}, bf16[160,8]{1,0:T(8,128)(2,1)}, bf16[1,256,768]{2,1,0:T(8,128)(2,1)}, bf16[1,256,768]{2,1,0:T(8,128)(2,1)}, bf16[1,768,256]{2,1,0:T(8,128)(2,1)}) custom-call(s32[160,8]{1,0:T(8,128)} %copy.12.ids_ref, bf16[160,8]{1,0:T(8,128)(2,1)} %copy.13.gate_ref, bf16[160,2048]{1,0:T(8,128)(2,1)} %tok_ref.1, ...), custom_call_target="tpu_custom_call" | custom-call | tf_op jit(solution)/shard_map/pallas_call | solution.py:345
  166.1 0.0 copy-start
  166.1 1.5 copy.14
  167.6 2.0 %copy.19 = bf16[160,2048]{1,0:T(8,128)(2,1)} copy(bf16[160,2048]{1,0:T(8,128)(2,1)} %get-tuple-element.15) | data formatting | bytes 1310720
  169.5 1.8 %copy.20 = bf16[1,256,768]{2,1,0:T(8,128)(2,1)} copy(bf16[1,256,768]{2,1,0:T(8,128)(2,1)} %get-tuple-element.17) | data formatting | bytes 786432
  171.3 1.8 %copy.21 = bf16[1,256,768]{2,1,0:T(8,128)(2,1)} copy(bf16[1,256,768]{2,1,0:T(8,128)(2,1)} %get-tuple-element.18) | data formatting | bytes 786432
  173.1 0.0 copy-done
  173.1 0.7 copy.22
Async XLA Ops:
  166.1 7.0 %copy-start = (bf16[1,768,256]{2,1,0:T(8,128)(2,1)S(1)}, bf16[1,768,256]{2,1,0:T(8,128)(2,1)}, u32[]{:S(2)}) copy-start(bf16[1,768,256]{2,1,0:T(8,128)(2,1)} %get-tuple-element.19) | copy-start | bytes 1179652

commit v2 on v1

--- a/solution.py
+++ b/solution.py
@@ -22,6 +22,9 @@
 UNITS = 6
 MSGS = 6
 HALF = 128
+FIRST = 14
+RELAYS = NE - FIRST
+CHUNKS = ((0, 224), (224, 144), (368, 144))
 
 
 def coords():
@@ -35,8 +38,11 @@
 
 
 def offset(j):
-    i = (j // 2) % 4
-    return i, (i + j // 8) % 4, j % 2
+    q, r = j // 2, (j - FIRST) // 2
+    plain = j < FIRST
+    dy = jnp.where(plain, jnp.where(q < 4, q, 0), 1 + r % 3)
+    kind = jnp.where(plain, jnp.where(q < 4, 0, q - 3), 1 + (r % 3 + r // 3) % 3)
+    return dy, kind, j % 2
 
 
 def z_shift(kind, core):
@@ -60,6 +66,14 @@
     x, y, z, c = coords()
     dy, kind, dc = offset(j)
     return (((y + dy) % 4) * 4 + (z + z_shift(kind, c) + 8) % 4) * 2 + (c + dc) % 2
+
+
+def turn(j, p, second):
+    x, y, z, c = coords()
+    dy, kind, dc = offset(j)
+    if second == (p == 0):
+        return device(x, y + dy, z, c)
+    return device(x, y, z + z_shift(kind, c), (c + dc) % 2)
 
 
 def peers():
@@ -85,8 +99,8 @@
 def kernel(
     ids_ref, gate_ref, tok_ref, dy_ref, wg_hbm, wu_hbm, wd_hbm,
     dtok_ref, dgate_ref, owg_ref, owu_ref, owd_ref,
-    wg, wu, wd, sent, xs, sel, gs, rt, back, dgs, rs_s, rs_r, own, z_s, z_r,
-    w_sem, d_ss, d_rs, b_ss, b_rs, r_ss, r_rs, z_ss, z_rs,
+    wg, wu, wd, sent, relay, xs, sel, gs, rt, back, dgs, rs_s, rs_r, own, z_s, z_r,
+    w_sem, h_ss, h_rs, d_ss, d_rs, b_ss, b_rs, r_ss, r_rs, z_ss, z_rs,
 ):
     x, y, z, c = coords()
     me = lax.axis_index("expert")
@@ -106,12 +120,14 @@
         load.start()
 
     expert_of = iota((TOK, GL), 1) // SLOT
+    ids = ids_ref[...].T
+    gates = gate_ref[...].astype(F32).T
     member = jnp.zeros((TOK, GL), F32)
     value = jnp.zeros((TOK, GL), F32)
     for k in range(TOP):
-        hit = ids_ref[:, k : k + 1] == expert_of
+        hit = ids[:, k : k + 1] == expert_of
         member = jnp.where(hit, 1.0, member)
-        value = jnp.where(hit, gate_ref[:, k : k + 1].astype(F32), value)
+        value = jnp.where(hit, gates[:, k : k + 1], value)
     earlier = (iota((TOK, TOK), 1) < iota((TOK, TOK), 0)).astype(F32).astype(BF)
     rank = jnp.dot(earlier, member.astype(BF), preferred_element_type=F32)
     slot_of = (iota((TOK, GL), 1) % SLOT).astype(F32)
@@ -130,30 +146,59 @@
 
     pl.semaphore_wait(barrier, count)
 
-    def dispatch(p, j):
+    def arrival(p, j, src, to):
         return pltpu.make_async_remote_copy(
-            src_ref=sent.at[p, block(target_expert(j))],
+            src_ref=src,
             dst_ref=xs.at[p, block(j)],
             send_sem=d_ss.at[p, j],
             recv_sem=d_rs.at[p, j],
-            device_id=target(j),
+            device_id=to,
             device_id_type=MESH,
         )
 
-    @pl.loop(1, NE)
+    def direct(p, j):
+        return arrival(p, j, sent.at[p, block(target_expert(j))], target(j))
+
+    def hop(p, r):
+        j = r + FIRST
+        return pltpu.make_async_remote_copy(
+            src_ref=sent.at[p, block(target_expert(j))],
+            dst_ref=relay.at[p, block(r)],
+            send_sem=h_ss.at[p, r],
+            recv_sem=h_rs.at[p, r],
+            device_id=turn(j, p, False),
+            device_id_type=MESH,
+        )
+
+    def onward(p, r):
+        j = r + FIRST
+        return arrival(p, j, relay.at[p, block(r)], turn(j, p, True))
+
+    @pl.loop(0, RELAYS)
+    def _(r):
+        hop(0, r).start()
+        hop(1, r).start()
+
+    @pl.loop(1, FIRST)
     def _(j):
-        dispatch(0, j).start()
-        dispatch(1, j).start()
+        direct(0, j).start()
+        direct(1, j).start()
 
     for p in range(2):
         xs[p, 0:SLOT, :] = sent[p, block(me), :]
     for load in loads:
         load.wait()
 
-    @pl.loop(1, NE)
+    @pl.loop(0, RELAYS)
+    def _(r):
+        for p in range(2):
+            hop(p, r).wait_recv()
+            onward(p, r).start()
+
+    @pl.loop(1, FIRST)
     def _(j):
-        dispatch(0, j).wait_recv()
-        dispatch(1, j).wait_recv()
+        direct(0, j).wait_recv()
+        direct(1, j).wait_recv()
 
     lane = iota((1, SLOT, GL), 2)
     mine = lane == me * SLOT + iota((1, SLOT, GL), 1)
@@ -187,9 +232,48 @@
         dgs[rows, :] = grads.astype(BF)
         xs[1, rows, :] = (scale * xs[1, rows, :].astype(F32)).astype(BF)
 
-    @pl.loop(0, 2)
-    def _(m):
-        expert(pl.ds(pl.multiple_of(m * 256, 256), 256), 256)
+    def input_rows(rows, count):
+        ends = iota((count, GL), 0) % SLOT == SLOT - 1
+
+        @pl.loop(0, D // 512)
+        def _(n):
+            feats = pl.ds(pl.multiple_of(n * 512, 512), 512)
+            contract = (((1,), (1,)), ((), ()))
+            out = lax.dot_general(gs[1, rows, :], wg[feats, :], contract, preferred_element_type=F32)
+            out = out + lax.dot_general(
+                gs[2, rows, :], wu[feats, :], contract, preferred_element_type=F32
+            )
+            rt[rows, feats] = out.astype(BF)
+
+        rt[rows, 0:GL] = jnp.where(ends, dgs[rows, :].astype(F32), rt[rows, 0:GL].astype(F32)).astype(BF)
+
+    def give_back(j):
+        return pltpu.make_async_remote_copy(
+            src_ref=rt.at[block(j)],
+            dst_ref=back.at[block(me)],
+            send_sem=b_ss.at[j],
+            recv_sem=b_rs.at[j],
+            device_id=origin(j),
+            device_id_type=MESH,
+        )
+
+    def return_blocks(start, count):
+        @pl.loop(max(start // SLOT, 1), (start + count) // SLOT)
+        def _(j):
+            give_back(j).start()
+
+    for n, (start, count) in enumerate(CHUNKS):
+        if n > 0:
+            @pl.loop(start // SLOT, (start + count) // SLOT)
+            def _(j):
+                onward(0, j - FIRST).wait_recv()
+                onward(1, j - FIRST).wait_recv()
+        if n == len(CHUNKS) - 1:
+            return_blocks(0, start)
+            back[block(me), :] = rt[0:SLOT, :]
+        expert(pl.ds(start, count), count)
+        if n < len(CHUNKS) - 1:
+            input_rows(pl.ds(start, count), count)
 
     def half_of(u):
         return jnp.where(u < 3, 1 - my_half, my_half)
@@ -231,35 +315,6 @@
             device_id_type=MESH,
         )
 
-    def give_back(j):
-        return pltpu.make_async_remote_copy(
-            src_ref=rt.at[block(j)],
-            dst_ref=back.at[block(me)],
-            send_sem=b_ss.at[j],
-            recv_sem=b_rs.at[j],
-            device_id=origin(j),
-            device_id_type=MESH,
-        )
-
-    def returns():
-        ends = iota((ROWS, 512), 0) % SLOT == SLOT - 1
-
-        @pl.loop(0, D // 512)
-        def _(n):
-            feats = pl.ds(pl.multiple_of(n * 512, 512), 512)
-            contract = (((1,), (1,)), ((), ()))
-            rows = lax.dot_general(gs[1], wg[feats, :], contract, preferred_element_type=F32)
-            rows = rows + lax.dot_general(gs[2], wu[feats, :], contract, preferred_element_type=F32)
-            rt[:, feats] = rows.astype(BF)
-
-        rt[:, 0:GL] = jnp.where(ends, dgs[...].astype(F32), rt[:, 0:GL].astype(F32)).astype(BF)
-
-        @pl.loop(1, NE)
-        def _(j):
-            give_back(j).start()
-
-        back[block(me), :] = rt[0:SLOT, :]
-
     @pl.loop(0, UNITS + 2)
     def _(v):
         @pl.when(v < UNITS)
@@ -272,7 +327,9 @@
 
         @pl.when(v == 1)
         def _():
-            returns()
+            start, count = CHUNKS[-1]
+            input_rows(pl.ds(start, count), count)
+            return_blocks(start, count)
 
         @pl.when((v >= 1) & (v < UNITS + 1))
         def _():
@@ -308,10 +365,10 @@
     at = iota((TOK, TOP), 1)
     grads = jnp.zeros((TOK, TOP), F32)
     for k in range(TOP):
-        hit = ids_ref[:, k : k + 1] == expert_of
+        hit = ids[:, k : k + 1] == expert_of
         one = jnp.sum(jnp.where(hit, picked, 0.0), axis=1, keepdims=True)
         grads = jnp.where(at == k, one, grads)
-    dgate_ref[...] = grads.astype(BF)
+    dgate_ref[...] = grads.T.astype(BF)
 
     for n, ref in enumerate((owd_ref, owg_ref, owu_ref)):
         for half in range(2):
@@ -324,9 +381,14 @@
 
     @pl.loop(1, NE)
     def _(j):
-        dispatch(0, j).wait_send()
-        dispatch(1, j).wait_send()
+        direct(0, j).wait_send()
+        direct(1, j).wait_send()
         give_back(j).wait_send()
+
+    @pl.loop(0, RELAYS)
+    def _(r):
+        hop(0, r).wait_send()
+        hop(1, r).wait_send()
 
     @pl.loop(0, UNITS)
     def _(u):
@@ -338,19 +400,34 @@
             to_partner(n, half).wait_send()
 
 
+def settle(*refs):
+    n = (len(refs) - 2) // 3
+    ins, outs, bufs, in_sem, out_sem = refs[:n], refs[n : 2 * n], refs[2 * n : 3 * n], refs[-2], refs[-1]
+    takes = [pltpu.make_async_copy(ins[i], bufs[i], in_sem.at[i]) for i in range(n)]
+    puts = [pltpu.make_async_copy(bufs[i], outs[i], out_sem.at[i]) for i in range(n)]
+    for take in takes:
+        take.start()
+    for take, put in zip(takes, puts):
+        take.wait()
+        put.start()
+    for put in puts:
+        put.wait()
+
+
 def body(tokens, out_grad, expert_ids, gate_vals, w_gate, w_up, w_down):
     vmem = pl.BlockSpec(memory_space=pltpu.VMEM)
     hbm = pl.BlockSpec(memory_space=pl.ANY)
     dma = pltpu.SemaphoreType.DMA
-    return pl.pallas_call(
+    shapes = (
+        jax.ShapeDtypeStruct((TOK, D), BF),
+        jax.ShapeDtypeStruct((TOP, TOK), BF),
+        jax.ShapeDtypeStruct((1, 256, FF), BF),
+        jax.ShapeDtypeStruct((1, 256, FF), BF),
+        jax.ShapeDtypeStruct((1, FF, 256), BF),
+    )
+    outs = pl.pallas_call(
         kernel,
-        out_shape=(
-            jax.ShapeDtypeStruct((TOK, D), BF),
-            jax.ShapeDtypeStruct((TOK, TOP), BF),
-            jax.ShapeDtypeStruct((1, 256, FF), BF),
-            jax.ShapeDtypeStruct((1, 256, FF), BF),
-            jax.ShapeDtypeStruct((1, FF, 256), BF),
-        ),
+        out_shape=shapes,
         in_specs=[vmem] * 4 + [hbm] * 3,
         out_specs=[vmem] * 5,
         scratch_shapes=[
@@ -358,6 +435,7 @@
             pltpu.VMEM((D, FF), BF),
             pltpu.VMEM((FF, D), BF),
             pltpu.VMEM((2, ROWS, D), BF),
+            pltpu.VMEM((2, RELAYS * SLOT, D), BF),
             pltpu.VMEM((2, ROWS, D), BF),
             pltpu.VMEM((TOK, GL), BF),
             pltpu.VMEM((3, ROWS, FF), BF),
@@ -370,6 +448,8 @@
             pltpu.VMEM((6, HALF, FF), BF),
             pltpu.VMEM((6, HALF, FF), BF),
             dma((3,)),
+            dma((2, RELAYS)),
+            dma((2, RELAYS)),
             dma((2, NE)),
             dma((2, NE)),
             dma((NE,)),
@@ -382,7 +462,16 @@
         compiler_params=pltpu.CompilerParams(
             collective_id=0, has_side_effects=True, vmem_limit_bytes=60 * 2**20
         ),
-    )(expert_ids, gate_vals, tokens, out_grad, w_gate, w_up, w_down)
+    )(expert_ids.T, gate_vals.T, tokens, out_grad, w_gate, w_up, w_down)
+    d_tokens, d_gates, d_gate, d_up, d_down = pl.pallas_call(
+        settle,
+        out_shape=shapes,
+        in_specs=[hbm] * 5,
+        out_specs=[hbm] * 5,
+        scratch_shapes=[pltpu.VMEM(s.shape, s.dtype) for s in shapes] + [dma((5,)), dma((5,))],
+        compiler_params=pltpu.CompilerParams(vmem_limit_bytes=60 * 2**20),
+    )(*outs)
+    return d_tokens, d_gates.T, d_gate, d_up, d_down
 
 
 def solution(mesh):

time: 174 us -> 153 us (0.88)
  the two profiles are of different devices: /device:TPU:69 before, /device:TPU:1 now
where the time goes in v2:
time: 153 us
  Pallas kernels  152 us (99%)
    pallas_call x1, Pallas kernels, body(): pl.pallas_call(kernel, out_shape=shapes, in_specs=[vmem] * 4 + [hbm] * 3,...  150 us

profile of v2, /device:TPU:1, one launch (start us, length us, event | category | flops | bytes accessed | tf_op | source)
XLA Modules:
  0.0 152.7 jit_solution(10494719584510700923)
XLA Ops:
  0.6 149.6 %shard_map.110 = (bf16[160,2048]{1,0:T(8,128)(2,1)}, bf16[8,160]{1,0:T(8,128)(2,1)}, bf16[1,256,768]{2,1,0:T(8,128)(2,1)}, bf16[1,256,768]{2,1,0:T(8,128)(2,1)}, bf16[1,768,256]{2,1,0:T(8,128)(2,1)}) custom-call(s32[8,160]{1,0:T(8,128)} %bitcast.3, bf16[8,160]{1,0:T(8,128)(2,1)} %bitcast.4, bf16[160,2048]{1,0:T(8,128)(2,1)} %tok_ref.1, ...), custom_call_target="tpu_custom_call" | custom-call | tf_op jit(solution)/shard_map/pallas_call | solution.py:428
  150.3 2.4 %shard_map.111 = (bf16[160,2048]{1,0:T(8,128)(2,1)}, bf16[8,160]{1,0:T(8,128)(2,1)}, bf16[1,256,768]{2,1,0:T(8,128)(2,1)}, bf16[1,256,768]{2,1,0:T(8,128)(2,1)}, bf16[1,768,256]{2,1,0:T(8,128)(2,1)}) custom-call(bf16[160,2048]{1,0:T(8,128)(2,1)} %get-tuple-element.15.refs_0_, bf16[8,160]{1,0:T(8,128)(2,1)} %get-tuple-element.16.refs_1_, ...), custom_call_target="tpu_custom_call" | custom-call | tf_op jit(solution)/shard_map/pallas_call | solution.py:466

commit v3 on v2

--- a/solution.py
+++ b/solution.py
@@ -24,7 +24,8 @@
 HALF = 128
 FIRST = 14
 RELAYS = NE - FIRST
-CHUNKS = ((0, 224), (224, 144), (368, 144))
+CHUNKS = ((0, 224), (224, 208), (432, 80))
+LAST = CHUNKS[2][0] // SLOT
 
 
 def coords():
@@ -97,9 +98,9 @@
 
 
 def kernel(
-    ids_ref, gate_ref, tok_ref, dy_ref, wg_hbm, wu_hbm, wd_hbm,
+    ids_hbm, gate_hbm, tok_hbm, dy_hbm, wg_hbm, wu_hbm, wd_hbm,
     dtok_ref, dgate_ref, owg_ref, owu_ref, owd_ref,
-    wg, wu, wd, sent, relay, xs, sel, gs, rt, back, dgs, rs_s, rs_r, own, z_s, z_r,
+    ids_ref, gate_ref, tok_ref, dy_ref, wg, wu, wd, sent, relay, xs, sel, gs, rt, back, dgs, rs_s, rs_r, own, z_s, z_r,
     w_sem, h_ss, h_rs, d_ss, d_rs, b_ss, b_rs, r_ss, r_rs, z_ss, z_rs,
 ):
     x, y, z, c = coords()
@@ -113,13 +114,17 @@
         count += 1
 
     loads = [
-        pltpu.make_async_copy(src.at[0], dst, w_sem.at[n])
-        for n, (src, dst) in enumerate(((wg_hbm, wg), (wu_hbm, wu), (wd_hbm, wd)))
+        pltpu.make_async_copy(src, dst, w_sem.at[n])
+        for n, (src, dst) in enumerate(
+            ((ids_hbm, ids_ref), (gate_hbm, gate_ref), (tok_hbm, tok_ref), (dy_hbm, dy_ref), (wg_hbm.at[0], wg), (wu_hbm.at[0], wu), (wd_hbm.at[0], wd))
+        )
     ]
     for load in loads:
         load.start()
 
     expert_of = iota((TOK, GL), 1) // SLOT
+    loads[0].wait()
+    loads[1].wait()
     ids = ids_ref[...].T
     gates = gate_ref[...].astype(F32).T
     member = jnp.zeros((TOK, GL), F32)
@@ -137,6 +142,7 @@
     pick = chosen.T.astype(BF)
     last = iota((ROWS, 512), 0) % SLOT == SLOT - 1
     for p, ref in enumerate((tok_ref, dy_ref)):
+        loads[2 + p].wait()
         for n in range(D // 512):
             cols = pl.ds(n * 512, 512)
             rows = jnp.dot(pick, ref[:, cols], preferred_element_type=F32)
@@ -150,8 +156,8 @@
         return pltpu.make_async_remote_copy(
             src_ref=src,
             dst_ref=xs.at[p, block(j)],
-            send_sem=d_ss.at[p, j],
-            recv_sem=d_rs.at[p, j],
+            send_sem=d_ss,
+            recv_sem=d_rs.at[jnp.where(j < FIRST, 0, jnp.where(j < LAST, 1, 2))],
             device_id=to,
             device_id_type=MESH,
         )
@@ -164,7 +170,7 @@
         return pltpu.make_async_remote_copy(
             src_ref=sent.at[p, block(target_expert(j))],
             dst_ref=relay.at[p, block(r)],
-            send_sem=h_ss.at[p, r],
+            send_sem=h_ss,
             recv_sem=h_rs.at[p, r],
             device_id=turn(j, p, False),
             device_id_type=MESH,
@@ -186,7 +192,7 @@
 
     for p in range(2):
         xs[p, 0:SLOT, :] = sent[p, block(me), :]
-    for load in loads:
+    for load in loads[4:]:
         load.wait()
 
     @pl.loop(0, RELAYS)
@@ -194,11 +200,6 @@
         for p in range(2):
             hop(p, r).wait_recv()
             onward(p, r).start()
-
-    @pl.loop(1, FIRST)
-    def _(j):
-        direct(0, j).wait_recv()
-        direct(1, j).wait_recv()
 
     lane = iota((1, SLOT, GL), 2)
     mine = lane == me * SLOT + iota((1, SLOT, GL), 1)
@@ -251,8 +252,8 @@
         return pltpu.make_async_remote_copy(
             src_ref=rt.at[block(j)],
             dst_ref=back.at[block(me)],
-            send_sem=b_ss.at[j],
-            recv_sem=b_rs.at[j],
+            send_sem=b_ss,
+            recv_sem=b_rs,
             device_id=origin(j),
             device_id_type=MESH,
         )
@@ -263,16 +264,14 @@
             give_back(j).start()
 
     for n, (start, count) in enumerate(CHUNKS):
-        if n > 0:
-            @pl.loop(start // SLOT, (start + count) // SLOT)
-            def _(j):
-                onward(0, j - FIRST).wait_recv()
-                onward(1, j - FIRST).wait_recv()
+        first = max(start, SLOT)
+        here = xs.at[:, pl.ds(first, start + count - first)]
+        pltpu.make_async_copy(here, here, d_rs.at[n]).wait()
         if n == len(CHUNKS) - 1:
-            return_blocks(0, start)
+            return_blocks(0, CHUNKS[0][1])
             back[block(me), :] = rt[0:SLOT, :]
         expert(pl.ds(start, count), count)
-        if n < len(CHUNKS) - 1:
+        if n == 0:
             input_rows(pl.ds(start, count), count)
 
     def half_of(u):
@@ -291,7 +290,7 @@
         return pltpu.make_async_remote_copy(
             src_ref=rs_s.at[u * MSGS + m],
             dst_ref=rs_r.at[u * MSGS + m],
-            send_sem=r_ss.at[u * MSGS + m],
+            send_sem=r_ss,
             recv_sem=r_rs.at[u * MSGS + m],
             device_id=device(x + step, y, z, c),
             device_id_type=MESH,
@@ -309,68 +308,32 @@
         return pltpu.make_async_remote_copy(
             src_ref=z_s.at[n * 2 + half],
             dst_ref=z_r.at[n * 2 + half],
-            send_sem=z_ss.at[n * 2 + half],
+            send_sem=z_ss,
             recv_sem=z_rs.at[n * 2 + half],
             device_id=device(x, y, z + 4, c),
             device_id_type=MESH,
         )
 
-    @pl.loop(0, UNITS + 2)
-    def _(v):
-        @pl.when(v < UNITS)
-        def _():
-            u = v
-            send(u, 0, tile(u, x + 2, 0))
-            send(u, 1, tile(u, x + 2, 1))
-            send(u, 2, tile(u, x + 1, 1))
-            send(u, 3, tile(u, x - 1, 0))
-
-        @pl.when(v == 1)
-        def _():
-            start, count = CHUNKS[-1]
-            input_rows(pl.ds(start, count), count)
-            return_blocks(start, count)
-
-        @pl.when((v >= 1) & (v < UNITS + 1))
-        def _():
-            u = v - 1
-            send(u, 4, tile(u, x + 1, 0) + received(u, 0))
-            send(u, 5, tile(u, x - 1, 1) + received(u, 1))
-
-        @pl.when(v >= 2)
-        def _():
-            u = v - 2
-            for half in range(2):
-                total = tile(u, x, half) + received(u, 4 + half) + received(u, 3 - half)
-
-                @pl.when(u < 3)
-                def _():
-                    z_s[u * 2 + half] = total.astype(BF)
-                    to_partner(u, half).start()
-
-                @pl.when(u >= 3)
-                def _():
-                    own[(u - 3) * 2 + half] = total
-
-    @pl.loop(1, NE)
-    def _(j):
-        give_back(j).wait_recv()
-
-    for n in range(D // 512):
-        cols = pl.ds(n * 512, 512)
-        dtok_ref[:, cols] = jnp.dot(sel[...], back[:, cols], preferred_element_type=F32).astype(BF)
-    ends = iota((ROWS, GL), 0) % SLOT == SLOT - 1
-    row = jnp.sum(jnp.where(ends, back[:, 0:GL].astype(F32), 0.0), axis=0, keepdims=True)
-    picked = sel[...].astype(F32) * row
-    at = iota((TOK, TOP), 1)
-    grads = jnp.zeros((TOK, TOP), F32)
-    for k in range(TOP):
-        hit = ids[:, k : k + 1] == expert_of
-        one = jnp.sum(jnp.where(hit, picked, 0.0), axis=1, keepdims=True)
-        grads = jnp.where(at == k, one, grads)
-    dgate_ref[...] = grads.T.astype(BF)
-
-    for n, ref in enumerate((owd_ref, owg_ref, owu_ref)):
+    def token_gradients():
+        others = back.at[pl.ds(SLOT, ROWS - SLOT)]
+        pltpu.make_async_copy(others, others, b_rs).wait()
+        for n in range(D // 512):
+            cols = pl.ds(n * 512, 512)
+            dtok_ref[:, cols] = jnp.dot(sel[...], back[:, cols], preferred_element_type=F32).astype(BF)
+        ends = iota((ROWS, GL), 0) % SLOT == SLOT - 1
+        row = jnp.sum(jnp.where(ends, back[:, 0:GL].astype(F32), 0.0), axis=0, keepdims=True)
+        picked = sel[...].astype(F32) * row
+        at = iota((TOK, TOP), 1)
+        named = ids_ref[...].T
+        grads = jnp.zeros((TOK, TOP), F32)
+        for k in range(TOP):
+            hit = named[:, k : k + 1] == iota((TOK, GL), 1) // SLOT
+            one = jnp.sum(jnp.where(hit, picked, 0.0), axis=1, keepdims=True)
+            grads = jnp.where(at == k, one, grads)
+        dgate_ref[...] = grads.T.astype(BF)
+
+    def finish(n):
+        ref = (owd_ref, owg_ref, owu_ref)[n]
         for half in range(2):
             to_partner(n, half).wait_recv()
             total = own[n * 2 + half] + z_r[n * 2 + half].astype(F32)
@@ -379,36 +342,68 @@
             else:
                 ref[0, half * HALF : (half + 1) * HALF, :] = total.astype(BF)
 
-    @pl.loop(1, NE)
-    def _(j):
-        direct(0, j).wait_send()
-        direct(1, j).wait_send()
-        give_back(j).wait_send()
-
-    @pl.loop(0, RELAYS)
-    def _(r):
-        hop(0, r).wait_send()
-        hop(1, r).wait_send()
-
-    @pl.loop(0, UNITS)
-    def _(u):
-        for m in range(MSGS):
-            message(u, m).wait_send()
-
-    for n in range(3):
-        for half in range(2):
-            to_partner(n, half).wait_send()
+    @pl.loop(0, UNITS + 2)
+    def _(v):
+        @pl.when(v < UNITS)
+        def _():
+            u = v
+            send(u, 0, tile(u, x + 2, 0))
+            send(u, 1, tile(u, x + 2, 1))
+            send(u, 2, tile(u, x + 1, 1))
+            send(u, 3, tile(u, x - 1, 0))
+
+        @pl.when(v == 1)
+        def _():
+            start = CHUNKS[1][0]
+            input_rows(pl.ds(start, ROWS - start), ROWS - start)
+            return_blocks(start, ROWS - start)
+
+        @pl.when(v == UNITS)
+        def _():
+            token_gradients()
+            finish(0)
+
+        @pl.when(v == UNITS + 1)
+        def _():
+            finish(1)
+
+        @pl.when((v >= 1) & (v < UNITS + 1))
+        def _():
+            u = v - 1
+            send(u, 4, tile(u, x + 1, 0) + received(u, 0))
+            send(u, 5, tile(u, x - 1, 1) + received(u, 1))
+
+        @pl.when(v >= 2)
+        def _():
+            u = v - 2
+            for half in range(2):
+                total = tile(u, x, half) + received(u, 4 + half) + received(u, 3 - half)
+
+                @pl.when(u < 3)
+                def _():
+                    z_s[u * 2 + half] = total.astype(BF)
+                    to_partner(u, half).start()
+
+                @pl.when(u >= 3)
+                def _():
+                    own[(u - 3) * 2 + half] = total
+
+    finish(2)
+
+    rest = pl.ds(SLOT, ROWS - SLOT)
+    for ref, sem in (
+        (xs.at[:, rest], d_ss), (relay, h_ss), (rt.at[rest], b_ss), (rs_s, r_ss), (z_s, z_ss),
+    ):
+        pltpu.make_async_remote_copy(
+            src_ref=ref, dst_ref=ref, send_sem=sem, recv_sem=sem,
+            device_id=device(x + 1, y, z, c), device_id_type=MESH,
+        ).wait_send()
 
 
 def settle(*refs):
-    n = (len(refs) - 2) // 3
-    ins, outs, bufs, in_sem, out_sem = refs[:n], refs[n : 2 * n], refs[2 * n : 3 * n], refs[-2], refs[-1]
-    takes = [pltpu.make_async_copy(ins[i], bufs[i], in_sem.at[i]) for i in range(n)]
-    puts = [pltpu.make_async_copy(bufs[i], outs[i], out_sem.at[i]) for i in range(n)]
-    for take in takes:
-        take.start()
-    for take, put in zip(takes, puts):
-        take.wait()
+    ins, outs, sem = refs[:5], refs[5:10], refs[10]
+    puts = [pltpu.make_async_copy(ins[i], outs[i], sem.at[i]) for i in range(5)]
+    for put in puts:
         put.start()
     for put in puts:
         put.wait()
@@ -428,9 +423,13 @@
     outs = pl.pallas_call(
         kernel,
         out_shape=shapes,
-        in_specs=[vmem] * 4 + [hbm] * 3,
+        in_specs=[pl.BlockSpec(memory_space=pltpu.HBM)] * 2 + [hbm] * 5,
         out_specs=[vmem] * 5,
         scratch_shapes=[
+            pltpu.VMEM((TOP, TOK), jnp.int32),
+            pltpu.VMEM((TOP, TOK), BF),
+            pltpu.VMEM((TOK, D), BF),
+            pltpu.VMEM((TOK, D), BF),
             pltpu.VMEM((D, FF), BF),
             pltpu.VMEM((D, FF), BF),
             pltpu.VMEM((FF, D), BF),
@@ -447,29 +446,29 @@
             pltpu.VMEM((6, HALF, FF), F32),
             pltpu.VMEM((6, HALF, FF), BF),
             pltpu.VMEM((6, HALF, FF), BF),
+            dma((7,)),
+            dma,
+            dma((2, RELAYS)),
+            dma,
             dma((3,)),
-            dma((2, RELAYS)),
-            dma((2, RELAYS)),
-            dma((2, NE)),
-            dma((2, NE)),
-            dma((NE,)),
-            dma((NE,)),
+            dma,
+            dma,
+            dma,
             dma((UNITS * MSGS,)),
-            dma((UNITS * MSGS,)),
-            dma((6,)),
+            dma,
             dma((6,)),
         ],
         compiler_params=pltpu.CompilerParams(
-            collective_id=0, has_side_effects=True, vmem_limit_bytes=60 * 2**20
+            collective_id=0, has_side_effects=True, vmem_limit_bytes=52 * 2**20
         ),
-    )(expert_ids.T, gate_vals.T, tokens, out_grad, w_gate, w_up, w_down)
+    )(pltpu.with_memory_space_constraint(expert_ids.T, pltpu.HBM), pltpu.with_memory_space_constraint(gate_vals.T, pltpu.HBM), tokens, out_grad, w_gate, w_up, w_down)
     d_tokens, d_gates, d_gate, d_up, d_down = pl.pallas_call(
         settle,
         out_shape=shapes,
         in_specs=[hbm] * 5,
         out_specs=[hbm] * 5,
-        scratch_shapes=[pltpu.VMEM(s.shape, s.dtype) for s in shapes] + [dma((5,)), dma((5,))],
-        compiler_params=pltpu.CompilerParams(vmem_limit_bytes=60 * 2**20),
+        scratch_shapes=[dma((5,))],
+        compiler_params=pltpu.CompilerParams(vmem_limit_bytes=2**20),
     )(*outs)
     return d_tokens, d_gates.T, d_gate, d_up, d_down
 

time: 153 us -> 151 us (0.987)
  the two profiles are of different devices: /device:TPU:1 before, /device:TPU:56 now
where the time goes in v3:
time: 151 us
  Pallas kernels  150 us (99%)
    pallas_call x1, Pallas kernels, body(): pl.pallas_call(kernel, out_shape=shapes, in_specs=[pl.BlockSpec(memory_sp...  149 us

profile of v3, /device:TPU:56, one launch (start us, length us, event | category | flops | bytes accessed | tf_op | source)
XLA Modules:
  0.0 151.1 jit_solution(14904204073403771141)
XLA Ops:
  0.6 149.2 %shard_map.110 = (bf16[160,2048]{1,0:T(8,128)(2,1)S(1)}, bf16[8,160]{1,0:T(8,128)(2,1)S(1)}, bf16[1,256,768]{2,1,0:T(8,128)(2,1)S(1)}, bf16[1,256,768]{2,1,0:T(8,128)(2,1)S(1)}, bf16[1,768,256]{2,1,0:T(8,128)(2,1)S(1)}) custom-call(s32[8,160]{1,0:T(8,128)} %bitcast.3, bf16[8,160]{1,0:T(8,128)(2,1)} %bitcast.4, bf16[160,2048]{1,0:T(8,128)(2,1)} %tok_hbm.1, ...), custom_call_target="tpu_custom_call" | custom-call | tf_op jit(solution)/shard_map/pallas_call | solution.py:423
  149.8 1.3 shard_map.111

commit v4 on v3

--- a/solution.py
+++ b/solution.py
@@ -24,7 +24,8 @@
 HALF = 128
 FIRST = 14
 RELAYS = NE - FIRST
-CHUNKS = ((0, 224), (224, 208), (432, 80))
+WIDTH = (D - 128, D)
+CHUNKS = ((0, 224), (224, 144), (368, 144))
 LAST = CHUNKS[2][0] // SLOT
 
 
@@ -140,37 +141,39 @@
     sel[...] = chosen.astype(BF)
     gate_row = jnp.sum(chosen * value, axis=0, keepdims=True)
     pick = chosen.T.astype(BF)
-    last = iota((ROWS, 512), 0) % SLOT == SLOT - 1
-    for p, ref in enumerate((tok_ref, dy_ref)):
-        loads[2 + p].wait()
-        for n in range(D // 512):
-            cols = pl.ds(n * 512, 512)
-            rows = jnp.dot(pick, ref[:, cols], preferred_element_type=F32)
-            if p == 0 and n == 0:
-                rows = jnp.where(last, gate_row, rows)
-            sent[p, :, cols] = rows.astype(BF)
+    at_end = iota((NE, SLOT, 128), 1) == SLOT - 1
+    loads[2].wait()
+    tail = jnp.dot(pick, tok_ref[:, WIDTH[0] :], preferred_element_type=F32).reshape(NE, SLOT, 128)
+    for n in range(4):
+        first, stop = n * 512, min(n * 512 + 512, WIDTH[0])
+        rows = jnp.dot(pick, tok_ref[:, first:stop], preferred_element_type=F32)
+        for k in range(0, stop - first, 128):
+            r = (first + k) // 128
+            part = rows[:, k : k + 128].reshape(NE, SLOT, 128)
+            part = jnp.where(at_end, tail[:, r : r + 1, :], part)
+            sent[0, :, first + k : first + k + 128] = part.reshape(ROWS, 128).astype(BF)
 
     pl.semaphore_wait(barrier, count)
 
     def arrival(p, j, src, to):
         return pltpu.make_async_remote_copy(
             src_ref=src,
-            dst_ref=xs.at[p, block(j)],
-            send_sem=d_ss,
-            recv_sem=d_rs.at[jnp.where(j < FIRST, 0, jnp.where(j < LAST, 1, 2))],
+            dst_ref=xs.at[p, block(j), 0 : WIDTH[p]],
+            send_sem=d_ss.at[p],
+            recv_sem=d_rs.at[p, jnp.where(j < FIRST, 0, jnp.where(j < LAST, 1, 2))],
             device_id=to,
             device_id_type=MESH,
         )
 
     def direct(p, j):
-        return arrival(p, j, sent.at[p, block(target_expert(j))], target(j))
+        return arrival(p, j, sent.at[p, block(target_expert(j)), 0 : WIDTH[p]], target(j))
 
     def hop(p, r):
         j = r + FIRST
         return pltpu.make_async_remote_copy(
-            src_ref=sent.at[p, block(target_expert(j))],
-            dst_ref=relay.at[p, block(r)],
-            send_sem=h_ss,
+            src_ref=sent.at[p, block(target_expert(j)), 0 : WIDTH[p]],
+            dst_ref=relay.at[p, block(r), 0 : WIDTH[p]],
+            send_sem=h_ss.at[p],
             recv_sem=h_rs.at[p, r],
             device_id=turn(j, p, False),
             device_id_type=MESH,
@@ -178,20 +181,35 @@
 
     def onward(p, r):
         j = r + FIRST
-        return arrival(p, j, relay.at[p, block(r)], turn(j, p, True))
+        return arrival(p, j, relay.at[p, block(r), 0 : WIDTH[p]], turn(j, p, True))
 
     @pl.loop(0, RELAYS)
     def _(r):
         hop(0, r).start()
-        hop(1, r).start()
 
     @pl.loop(1, FIRST)
     def _(j):
         direct(0, j).start()
+
+    last = iota((ROWS, 512), 0) % SLOT == SLOT - 1
+    loads[3].wait()
+    for n in range(D // 512):
+        cols = pl.ds(n * 512, 512)
+        rows = jnp.dot(pick, dy_ref[:, cols], preferred_element_type=F32)
+        if n == 0:
+            rows = jnp.where(last, gate_row, rows)
+        sent[1, :, cols] = rows.astype(BF)
+
+    @pl.loop(0, RELAYS)
+    def _(r):
+        hop(1, r).start()
+
+    @pl.loop(1, FIRST)
+    def _(j):
         direct(1, j).start()
 
     for p in range(2):
-        xs[p, 0:SLOT, :] = sent[p, block(me), :]
+        xs[p, 0:SLOT, 0 : WIDTH[p]] = sent[p, block(me), 0 : WIDTH[p]]
     for load in loads[4:]:
         load.wait()
 
@@ -205,7 +223,13 @@
     mine = lane == me * SLOT + iota((1, SLOT, GL), 1)
 
     def expert(rows, count):
-        row = xs[0, rows, 0:GL].astype(F32).reshape(count // SLOT, SLOT, GL)
+        place = iota((1, SLOT, 128), 1)
+        tail = jnp.zeros((count // SLOT, SLOT, 128), F32)
+        for r in range(SLOT - 1):
+            part = xs[0, rows, r * 128 : (r + 1) * 128].astype(F32).reshape(count // SLOT, SLOT, 128)
+            tail = jnp.where(place == r, part[:, SLOT - 1 : SLOT, :], tail)
+        xs[0, rows, WIDTH[0] :] = tail.reshape(count, 128).astype(BF)
+        row = xs[1, rows, 0:GL].astype(F32).reshape(count // SLOT, SLOT, GL)
         row = jnp.where(iota((1, SLOT, GL), 1) == SLOT - 1, row, 0.0)
         row = jnp.sum(row, axis=1, keepdims=True)
         scale = jnp.sum(jnp.where(mine, row, 0.0), axis=2, keepdims=True).reshape(count, 1)
@@ -265,13 +289,14 @@
 
     for n, (start, count) in enumerate(CHUNKS):
         first = max(start, SLOT)
-        here = xs.at[:, pl.ds(first, start + count - first)]
-        pltpu.make_async_copy(here, here, d_rs.at[n]).wait()
+        for p in range(2):
+            here = xs.at[p, pl.ds(first, start + count - first), 0 : WIDTH[p]]
+            pltpu.make_async_copy(here, here, d_rs.at[p, n]).wait()
         if n == len(CHUNKS) - 1:
-            return_blocks(0, CHUNKS[0][1])
+            return_blocks(0, start)
             back[block(me), :] = rt[0:SLOT, :]
         expert(pl.ds(start, count), count)
-        if n == 0:
+        if n < 2:
             input_rows(pl.ds(start, count), count)
 
     def half_of(u):
@@ -349,12 +374,10 @@
             u = v
             send(u, 0, tile(u, x + 2, 0))
             send(u, 1, tile(u, x + 2, 1))
-            send(u, 2, tile(u, x + 1, 1))
-            send(u, 3, tile(u, x - 1, 0))
 
         @pl.when(v == 1)
         def _():
-            start = CHUNKS[1][0]
+            start = CHUNKS[2][0]
             input_rows(pl.ds(start, ROWS - start), ROWS - start)
             return_blocks(start, ROWS - start)
 
@@ -372,6 +395,12 @@
             u = v - 1
             send(u, 4, tile(u, x + 1, 0) + received(u, 0))
             send(u, 5, tile(u, x - 1, 1) + received(u, 1))
+
+        @pl.when(v < UNITS)
+        def _():
+            u = v
+            send(u, 2, tile(u, x + 1, 1))
+            send(u, 3, tile(u, x - 1, 0))
 
         @pl.when(v >= 2)
         def _():
@@ -392,7 +421,8 @@
 
     rest = pl.ds(SLOT, ROWS - SLOT)
     for ref, sem in (
-        (xs.at[:, rest], d_ss), (relay, h_ss), (rt.at[rest], b_ss), (rs_s, r_ss), (z_s, z_ss),
+        (xs.at[0, rest, 0 : WIDTH[0]], d_ss.at[0]), (xs.at[1, rest], d_ss.at[1]),
+        (relay.at[0, :, 0 : WIDTH[0]], h_ss.at[0]), (relay.at[1], h_ss.at[1]), (rt.at[rest], b_ss), (rs_s, r_ss), (z_s, z_ss),
     ):
         pltpu.make_async_remote_copy(
             src_ref=ref, dst_ref=ref, send_sem=sem, recv_sem=sem,
@@ -447,10 +477,10 @@
             pltpu.VMEM((6, HALF, FF), BF),
             pltpu.VMEM((6, HALF, FF), BF),
             dma((7,)),
-            dma,
+            dma((2,)),
             dma((2, RELAYS)),
-            dma,
-            dma((3,)),
+            dma((2,)),
+            dma((2, 3)),
             dma,
             dma,
             dma,

time: 151 us -> 143 us (0.947)
  the two profiles are of different devices: /device:TPU:56 before, /device:TPU:1 now
where the time goes in v4:
time: 143 us
  Pallas kernels  143 us (100%)
    pallas_call x1, Pallas kernels, body(): pl.pallas_call(kernel, out_shape=shapes, in_specs=[pl.BlockSpec(memory_sp...  141 us

profile of v4, /device:TPU:1, one launch (start us, length us, event | category | flops | bytes accessed | tf_op | source)
XLA Modules:
  0.0 143.2 jit_solution(3944805957412086144)
XLA Ops:
  0.6 141.3 %shard_map.110 = (bf16[160,2048]{1,0:T(8,128)(2,1)S(1)}, bf16[8,160]{1,0:T(8,128)(2,1)S(1)}, bf16[1,256,768]{2,1,0:T(8,128)(2,1)S(1)}, bf16[1,256,768]{2,1,0:T(8,128)(2,1)S(1)}, bf16[1,768,256]{2,1,0:T(8,128)(2,1)S(1)}) custom-call(s32[8,160]{1,0:T(8,128)} %bitcast.3, bf16[8,160]{1,0:T(8,128)(2,1)} %bitcast.4, bf16[160,2048]{1,0:T(8,128)(2,1)} %tok_hbm.1, ...), custom_call_target="tpu_custom_call" | custom-call | tf_op jit(solution)/shard_map/pallas_call | solution.py:453
  141.9 1.3 shard_map.111

commit v5 on v4

--- a/solution.py
+++ b/solution.py
@@ -24,7 +24,7 @@
 HALF = 128
 FIRST = 14
 RELAYS = NE - FIRST
-WIDTH = (D - 128, D)
+WIDTH = D - 128
 CHUNKS = ((0, 224), (224, 144), (368, 144))
 LAST = CHUNKS[2][0] // SLOT
 
@@ -80,8 +80,8 @@
 
 def peers():
     x, y, z, c = coords()
-    for dz in (0, 1, -1, 2, -2):
-        for dy in range(4):
+    for dz in (2, -2, 1, -1, 0):
+        for dy in (2, 1, 3, 0):
             for dc in (0, 1):
                 if (dz, dy, dc) != (0, 0, 0):
                     yield device(x, y + dy, z + dz, (c + dc) % 2)
@@ -101,7 +101,7 @@
 def kernel(
     ids_hbm, gate_hbm, tok_hbm, dy_hbm, wg_hbm, wu_hbm, wd_hbm,
     dtok_ref, dgate_ref, owg_ref, owu_ref, owd_ref,
-    ids_ref, gate_ref, tok_ref, dy_ref, wg, wu, wd, sent, relay, xs, sel, gs, rt, back, dgs, rs_s, rs_r, own, z_s, z_r,
+    ids_ref, gate_ref, tok_ref, dy_ref, wg, wu, wd, pre, sent, relay, xs, sel, gs, rt, back, dgs, rs_s, rs_r, own, z_s, z_r,
     w_sem, h_ss, h_rs, d_ss, d_rs, b_ss, b_rs, r_ss, r_rs, z_ss, z_rs,
 ):
     x, y, z, c = coords()
@@ -139,26 +139,29 @@
     slot_of = (iota((TOK, GL), 1) % SLOT).astype(F32)
     chosen = jnp.where(rank == slot_of, member, 0.0)
     sel[...] = chosen.astype(BF)
-    gate_row = jnp.sum(chosen * value, axis=0, keepdims=True)
-    pick = chosen.T.astype(BF)
+    picks = chosen.T.astype(BF), (chosen * value).T.astype(BF)
     at_end = iota((NE, SLOT, 128), 1) == SLOT - 1
+
+    def pack(p, ref):
+        tail = jnp.dot(picks[p], ref[:, WIDTH:], preferred_element_type=F32).reshape(NE, SLOT, 128)
+        for n in range(4):
+            first, stop = n * 512, min(n * 512 + 512, WIDTH)
+            rows = jnp.dot(picks[p], ref[:, first:stop], preferred_element_type=F32)
+            for k in range(0, stop - first, 128):
+                r = (first + k) // 128
+                part = rows[:, k : k + 128].reshape(NE, SLOT, 128)
+                part = jnp.where(at_end, tail[:, r : r + 1, :], part)
+                sent[p, :, first + k : first + k + 128] = part.reshape(ROWS, 128).astype(BF)
+
     loads[2].wait()
-    tail = jnp.dot(pick, tok_ref[:, WIDTH[0] :], preferred_element_type=F32).reshape(NE, SLOT, 128)
-    for n in range(4):
-        first, stop = n * 512, min(n * 512 + 512, WIDTH[0])
-        rows = jnp.dot(pick, tok_ref[:, first:stop], preferred_element_type=F32)
-        for k in range(0, stop - first, 128):
-            r = (first + k) // 128
-            part = rows[:, k : k + 128].reshape(NE, SLOT, 128)
-            part = jnp.where(at_end, tail[:, r : r + 1, :], part)
-            sent[0, :, first + k : first + k + 128] = part.reshape(ROWS, 128).astype(BF)
+    pack(0, tok_ref)
 
     pl.semaphore_wait(barrier, count)
 
     def arrival(p, j, src, to):
         return pltpu.make_async_remote_copy(
             src_ref=src,
-            dst_ref=xs.at[p, block(j), 0 : WIDTH[p]],
+            dst_ref=xs.at[p, block(j), 0 : WIDTH],
             send_sem=d_ss.at[p],
             recv_sem=d_rs.at[p, jnp.where(j < FIRST, 0, jnp.where(j < LAST, 1, 2))],
             device_id=to,
@@ -166,13 +169,13 @@
         )
 
     def direct(p, j):
-        return arrival(p, j, sent.at[p, block(target_expert(j)), 0 : WIDTH[p]], target(j))
+        return arrival(p, j, sent.at[p, block(target_expert(j)), 0 : WIDTH], target(j))
 
     def hop(p, r):
         j = r + FIRST
         return pltpu.make_async_remote_copy(
-            src_ref=sent.at[p, block(target_expert(j)), 0 : WIDTH[p]],
-            dst_ref=relay.at[p, block(r), 0 : WIDTH[p]],
+            src_ref=sent.at[p, block(target_expert(j)), 0 : WIDTH],
+            dst_ref=relay.at[p, block(r), 0 : WIDTH],
             send_sem=h_ss.at[p],
             recv_sem=h_rs.at[p, r],
             device_id=turn(j, p, False),
@@ -181,7 +184,7 @@
 
     def onward(p, r):
         j = r + FIRST
-        return arrival(p, j, relay.at[p, block(r), 0 : WIDTH[p]], turn(j, p, True))
+        return arrival(p, j, relay.at[p, block(r), 0 : WIDTH], turn(j, p, True))
 
     @pl.loop(0, RELAYS)
     def _(r):
@@ -191,14 +194,8 @@
     def _(j):
         direct(0, j).start()
 
-    last = iota((ROWS, 512), 0) % SLOT == SLOT - 1
     loads[3].wait()
-    for n in range(D // 512):
-        cols = pl.ds(n * 512, 512)
-        rows = jnp.dot(pick, dy_ref[:, cols], preferred_element_type=F32)
-        if n == 0:
-            rows = jnp.where(last, gate_row, rows)
-        sent[1, :, cols] = rows.astype(BF)
+    pack(1, dy_ref)
 
     @pl.loop(0, RELAYS)
     def _(r):
@@ -209,7 +206,7 @@
         direct(1, j).start()
 
     for p in range(2):
-        xs[p, 0:SLOT, 0 : WIDTH[p]] = sent[p, block(me), 0 : WIDTH[p]]
+        xs[p, 0:SLOT, 0 : WIDTH] = sent[p, block(me), 0 : WIDTH]
     for load in loads[4:]:
         load.wait()
 
@@ -222,40 +219,47 @@
     lane = iota((1, SLOT, GL), 2)
     mine = lane == me * SLOT + iota((1, SLOT, GL), 1)
 
-    def expert(rows, count):
+    def live(count):
+        return iota((count, 1), 0) % SLOT < SLOT - 1
+
+    def forward(rows, count):
         place = iota((1, SLOT, 128), 1)
-        tail = jnp.zeros((count // SLOT, SLOT, 128), F32)
-        for r in range(SLOT - 1):
-            part = xs[0, rows, r * 128 : (r + 1) * 128].astype(F32).reshape(count // SLOT, SLOT, 128)
-            tail = jnp.where(place == r, part[:, SLOT - 1 : SLOT, :], tail)
-        xs[0, rows, WIDTH[0] :] = tail.reshape(count, 128).astype(BF)
-        row = xs[1, rows, 0:GL].astype(F32).reshape(count // SLOT, SLOT, GL)
-        row = jnp.where(iota((1, SLOT, GL), 1) == SLOT - 1, row, 0.0)
-        row = jnp.sum(row, axis=1, keepdims=True)
-        scale = jnp.sum(jnp.where(mine, row, 0.0), axis=2, keepdims=True).reshape(count, 1)
-
-        def part(f, total):
+        for p in range(2):
+            tail = jnp.zeros((count // SLOT, SLOT, 128), F32)
+            for r in range(SLOT - 1):
+                part = xs[p, rows, r * 128 : (r + 1) * 128].astype(F32)
+                part = part.reshape(count // SLOT, SLOT, 128)
+                tail = jnp.where(place == r, part[:, SLOT - 1 : SLOT, :], tail)
+            xs[p, rows, WIDTH:] = tail.reshape(count, 128).astype(BF)
+
+        @pl.loop(0, FF // 256)
+        def _(f):
             cols = pl.ds(pl.multiple_of(f * 256, 256), 256)
             gate_pre = jnp.dot(xs[0, rows, :], wg[:, cols], preferred_element_type=F32)
             up_pre = jnp.dot(xs[0, rows, :], wu[:, cols], preferred_element_type=F32)
-            raw = lax.dot_general(
+            pre[0, 0:count, cols] = gate_pre
+            pre[1, 0:count, cols] = up_pre
+            hidden = gate_pre * jax.nn.sigmoid(gate_pre) * up_pre
+            gs[0, rows, cols] = jnp.where(live(count), hidden, 0.0).astype(BF)
+
+    def backward(rows, count):
+        def part(f, total):
+            cols = pl.ds(pl.multiple_of(f * 256, 256), 256)
+            grad = lax.dot_general(
                 xs[1, rows, :], wd[cols, :], (((1,), (1,)), ((), ())), preferred_element_type=F32
             )
+            grad = jnp.where(live(count), grad, 0.0)
+            gate_pre, up_pre = pre[0, 0:count, cols], pre[1, 0:count, cols]
             sig = jax.nn.sigmoid(gate_pre)
-            silu = gate_pre * sig
-            hidden = (silu * up_pre).astype(BF)
-            grad = scale * raw
-            gs[2, rows, cols] = (grad * silu).astype(BF)
+            gs[2, rows, cols] = (grad * gate_pre * sig).astype(BF)
             gs[1, rows, cols] = (grad * up_pre * sig * (1.0 + gate_pre * (1.0 - sig))).astype(BF)
-            gs[0, rows, cols] = hidden
-            return total + jnp.sum(hidden.astype(F32) * raw, axis=1, keepdims=True)
+            return total + jnp.sum(gs[0, rows, cols].astype(F32) * grad, axis=1, keepdims=True)
 
         total = lax.fori_loop(0, FF // 256, part, jnp.zeros((count, 1), F32))
         grads = total.astype(BF).astype(F32).reshape(count // SLOT, SLOT, 1)
         grads = jnp.sum(jnp.where(mine, grads, 0.0), axis=1, keepdims=True)
         grads = jnp.broadcast_to(grads, (count // SLOT, SLOT, GL)).reshape(count, GL)
         dgs[rows, :] = grads.astype(BF)
-        xs[1, rows, :] = (scale * xs[1, rows, :].astype(F32)).astype(BF)
 
     def input_rows(rows, count):
         ends = iota((count, GL), 0) % SLOT == SLOT - 1
@@ -290,12 +294,14 @@
     for n, (start, count) in enumerate(CHUNKS):
         first = max(start, SLOT)
         for p in range(2):
-            here = xs.at[p, pl.ds(first, start + count - first), 0 : WIDTH[p]]
+            here = xs.at[p, pl.ds(first, start + count - first), 0 : WIDTH]
             pltpu.make_async_copy(here, here, d_rs.at[p, n]).wait()
         if n == len(CHUNKS) - 1:
             return_blocks(0, start)
             back[block(me), :] = rt[0:SLOT, :]
-        expert(pl.ds(start, count), count)
+        forward(pl.ds(start, count), count)
+        if n < 2:
+            backward(pl.ds(start, count), count)
         if n < 2:
             input_rows(pl.ds(start, count), count)
 
@@ -350,12 +356,13 @@
         picked = sel[...].astype(F32) * row
         at = iota((TOK, TOP), 1)
         named = ids_ref[...].T
+        weights = gate_ref[...].astype(F32).T
         grads = jnp.zeros((TOK, TOP), F32)
         for k in range(TOP):
             hit = named[:, k : k + 1] == iota((TOK, GL), 1) // SLOT
             one = jnp.sum(jnp.where(hit, picked, 0.0), axis=1, keepdims=True)
             grads = jnp.where(at == k, one, grads)
-        dgate_ref[...] = grads.T.astype(BF)
+        dgate_ref[...] = (grads / weights).T.astype(BF)
 
     def finish(n):
         ref = (owd_ref, owg_ref, owu_ref)[n]
@@ -402,6 +409,10 @@
             send(u, 2, tile(u, x + 1, 1))
             send(u, 3, tile(u, x - 1, 0))
 
+        @pl.when(v == 0)
+        def _():
+            backward(pl.ds(CHUNKS[2][0], CHUNKS[2][1]), CHUNKS[2][1])
+
         @pl.when(v >= 2)
         def _():
             u = v - 2
@@ -421,8 +432,8 @@
 
     rest = pl.ds(SLOT, ROWS - SLOT)
     for ref, sem in (
-        (xs.at[0, rest, 0 : WIDTH[0]], d_ss.at[0]), (xs.at[1, rest], d_ss.at[1]),
-        (relay.at[0, :, 0 : WIDTH[0]], h_ss.at[0]), (relay.at[1], h_ss.at[1]), (rt.at[rest], b_ss), (rs_s, r_ss), (z_s, z_ss),
+        (xs.at[0, rest, 0 : WIDTH], d_ss.at[0]), (xs.at[1, rest, 0:WIDTH], d_ss.at[1]),
+        (relay.at[0, :, 0 : WIDTH], h_ss.at[0]), (relay.at[1, :, 0:WIDTH], h_ss.at[1]), (rt.at[rest], b_ss), (rs_s, r_ss), (z_s, z_ss),
     ):
         pltpu.make_async_remote_copy(
             src_ref=ref, dst_ref=ref, send_sem=sem, recv_sem=sem,
@@ -463,6 +474,7 @@
             pltpu.VMEM((D, FF), BF),
             pltpu.VMEM((D, FF), BF),
             pltpu.VMEM((FF, D), BF),
+            pltpu.VMEM((2, CHUNKS[0][1], FF), F32),
             pltpu.VMEM((2, ROWS, D), BF),
             pltpu.VMEM((2, RELAYS * SLOT, D), BF),
             pltpu.VMEM((2, ROWS, D), BF),

time: 143 us -> 141 us (0.986)
  Pallas kernels: 143 us -> 140 us
    pallas_call x1, Pallas kernels: 141 us -> 139 us  [body(): pl.pallas_call(kernel, out_shape=shapes, in_specs=[pl.BlockSpec(memory_sp...]
where the time goes in v5:
time: 141 us
  Pallas kernels  140 us (99%)
    pallas_call x1, Pallas kernels, body(): pl.pallas_call(kernel, out_shape=shapes, in_specs=[pl.BlockSpec(memory_sp...  139 us

profile of v5, /device:TPU:1, one launch (start us, length us, event | category | flops | bytes accessed | tf_op | source)
XLA Modules:
  0.0 140.9 jit_solution(7043554442341308501)
XLA Ops:
  0.6 139.0 %shard_map.110 = (bf16[160,2048]{1,0:T(8,128)(2,1)S(1)}, bf16[8,160]{1,0:T(8,128)(2,1)S(1)}, bf16[1,256,768]{2,1,0:T(8,128)(2,1)S(1)}, bf16[1,256,768]{2,1,0:T(8,128)(2,1)S(1)}, bf16[1,768,256]{2,1,0:T(8,128)(2,1)S(1)}) custom-call(s32[8,160]{1,0:T(8,128)} %bitcast.3, bf16[8,160]{1,0:T(8,128)(2,1)} %bitcast.4, bf16[160,2048]{1,0:T(8,128)(2,1)} %tok_hbm.1, ...), custom_call_target="tpu_custom_call" | custom-call | tf_op jit(solution)/shard_map/pallas_call | solution.py:464
  139.7 1.3 shard_map.111

commit v6 on v5

--- a/solution.py
+++ b/solution.py
@@ -101,7 +101,7 @@
 def kernel(
     ids_hbm, gate_hbm, tok_hbm, dy_hbm, wg_hbm, wu_hbm, wd_hbm,
     dtok_ref, dgate_ref, owg_ref, owu_ref, owd_ref,
-    ids_ref, gate_ref, tok_ref, dy_ref, wg, wu, wd, pre, sent, relay, xs, sel, gs, rt, back, dgs, rs_s, rs_r, own, z_s, z_r,
+    ids_ref, gate_ref, tok_ref, dy_ref, wg, wu, wd, pre, sent, relay, xs, taken, sel, gs, rt, back, dgs, rs_s, rs_r, own, z_s, z_r,
     w_sem, h_ss, h_rs, d_ss, d_rs, b_ss, b_rs, r_ss, r_rs, z_ss, z_rs,
 ):
     x, y, z, c = coords()
@@ -123,23 +123,21 @@
     for load in loads:
         load.start()
 
-    expert_of = iota((TOK, GL), 1) // SLOT
     loads[0].wait()
     loads[1].wait()
-    ids = ids_ref[...].T
-    gates = gate_ref[...].astype(F32).T
-    member = jnp.zeros((TOK, GL), F32)
-    value = jnp.zeros((TOK, GL), F32)
+    expert_of = iota((GL, TOK), 0) // SLOT
+    member = jnp.zeros((GL, TOK), F32)
+    value = jnp.zeros((GL, TOK), F32)
     for k in range(TOP):
-        hit = ids[:, k : k + 1] == expert_of
+        hit = ids_ref[k : k + 1, :] == expert_of
         member = jnp.where(hit, 1.0, member)
-        value = jnp.where(hit, gates[:, k : k + 1], value)
-    earlier = (iota((TOK, TOK), 1) < iota((TOK, TOK), 0)).astype(F32).astype(BF)
-    rank = jnp.dot(earlier, member.astype(BF), preferred_element_type=F32)
-    slot_of = (iota((TOK, GL), 1) % SLOT).astype(F32)
+        value = jnp.where(hit, gate_ref[k : k + 1, :].astype(F32), value)
+    earlier = (iota((TOK, TOK), 0) < iota((TOK, TOK), 1)).astype(F32).astype(BF)
+    rank = jnp.dot(member.astype(BF), earlier, preferred_element_type=F32)
+    slot_of = (iota((GL, TOK), 0) % SLOT).astype(F32)
     chosen = jnp.where(rank == slot_of, member, 0.0)
-    sel[...] = chosen.astype(BF)
-    picks = chosen.T.astype(BF), (chosen * value).T.astype(BF)
+    picks = chosen.astype(BF), (chosen * value).astype(BF)
+    taken[...] = picks[0]
     at_end = iota((NE, SLOT, 128), 1) == SLOT - 1
 
     def pack(p, ref):
@@ -215,6 +213,8 @@
         for p in range(2):
             hop(p, r).wait_recv()
             onward(p, r).start()
+
+    sel[...] = taken[...].astype(F32).T.astype(BF)
 
     lane = iota((1, SLOT, GL), 2)
     mine = lane == me * SLOT + iota((1, SLOT, GL), 1)
@@ -478,6 +478,7 @@
             pltpu.VMEM((2, ROWS, D), BF),
             pltpu.VMEM((2, RELAYS * SLOT, D), BF),
             pltpu.VMEM((2, ROWS, D), BF),
+            pltpu.VMEM((GL, TOK), BF),
             pltpu.VMEM((TOK, GL), BF),
             pltpu.VMEM((3, ROWS, FF), BF),
             pltpu.VMEM((ROWS, D), BF),

time: 141 us -> 141 us (level)
  no operation moved by 1% of the time
where the time goes in v6:
time: 141 us
  Pallas kernels  140 us (99%)
    pallas_call x1, Pallas kernels, body(): pl.pallas_call(kernel, out_shape=shapes, in_specs=[pl.BlockSpec(memory_sp...  139 us

profile of v6, /device:TPU:1, one launch (start us, length us, event | category | flops | bytes accessed | tf_op | source)
XLA Modules:
  0.0 140.9 jit_solution(16978836713409620689)
XLA Ops:
  0.6 139.0 %shard_map.110 = (bf16[160,2048]{1,0:T(8,128)(2,1)S(1)}, bf16[8,160]{1,0:T(8,128)(2,1)S(1)}, bf16[1,256,768]{2,1,0:T(8,128)(2,1)S(1)}, bf16[1,256,768]{2,1,0:T(8,128)(2,1)S(1)}, bf16[1,768,256]{2,1,0:T(8,128)(2,1)S(1)}) custom-call(s32[8,160]{1,0:T(8,128)} %bitcast.3, bf16[8,160]{1,0:T(8,128)(2,1)} %bitcast.4, bf16[160,2048]{1,0:T(8,128)(2,1)} %tok_hbm.1, ...), custom_call_target="tpu_custom_call" | custom-call | tf_op jit(solution)/shard_map/pallas_call | solution.py:464
  139.7 1.3 shard_map.111

commit v7 on v6

--- a/solution.py
+++ b/solution.py
@@ -175,7 +175,7 @@
             src_ref=sent.at[p, block(target_expert(j)), 0 : WIDTH],
             dst_ref=relay.at[p, block(r), 0 : WIDTH],
             send_sem=h_ss.at[p],
-            recv_sem=h_rs.at[p, r],
+            recv_sem=h_rs.at[p, r // 2],
             device_id=turn(j, p, False),
             device_id_type=MESH,
         )
@@ -208,11 +208,13 @@
     for load in loads[4:]:
         load.wait()
 
-    @pl.loop(0, RELAYS)
-    def _(r):
+    @pl.loop(0, RELAYS // 2)
+    def _(q):
         for p in range(2):
-            hop(p, r).wait_recv()
-            onward(p, r).start()
+            both = relay.at[p, pl.ds(pl.multiple_of(q * 2 * SLOT, 2 * SLOT), 2 * SLOT), 0:WIDTH]
+            pltpu.make_async_copy(both, both, h_rs.at[p, q]).wait()
+            onward(p, q * 2).start()
+            onward(p, q * 2 + 1).start()
 
     sel[...] = taken[...].astype(F32).T.astype(BF)
 
@@ -322,7 +324,7 @@
             src_ref=rs_s.at[u * MSGS + m],
             dst_ref=rs_r.at[u * MSGS + m],
             send_sem=r_ss,
-            recv_sem=r_rs.at[u * MSGS + m],
+            recv_sem=r_rs.at[u * 3 + min(m, 2)],
             device_id=device(x + step, y, z, c),
             device_id_type=MESH,
         )
@@ -416,8 +418,11 @@
         @pl.when(v >= 2)
         def _():
             u = v - 2
+            four = rs_r.at[pl.ds(u * MSGS + 2, 4)]
+            pltpu.make_async_copy(four, four, r_rs.at[u * 3 + 2]).wait()
             for half in range(2):
-                total = tile(u, x, half) + received(u, 4 + half) + received(u, 3 - half)
+                got = rs_r[u * MSGS + 4 + half].astype(F32) + rs_r[u * MSGS + 3 - half].astype(F32)
+                total = tile(u, x, half) + got
 
                 @pl.when(u < 3)
                 def _():
@@ -491,13 +496,13 @@
             pltpu.VMEM((6, HALF, FF), BF),
             dma((7,)),
             dma((2,)),
-            dma((2, RELAYS)),
+            dma((2, RELAYS // 2)),
             dma((2,)),
             dma((2, 3)),
             dma,
             dma,
             dma,
-            dma((UNITS * MSGS,)),
+            dma((UNITS * 3,)),
             dma,
             dma((6,)),
         ],

time: 141 us -> 144 us (1.021)
  the two profiles are of different devices: /device:TPU:1 before, /device:TPU:194 now
where the time goes in v7:
time: 144 us
  Pallas kernels  143 us (99%)
    pallas_call x1, Pallas kernels, body(): pl.pallas_call(kernel, out_shape=shapes, in_specs=[pl.BlockSpec(memory_sp...  142 us

profile of v7, /device:TPU:194, one launch (start us, length us, event | category | flops | bytes accessed | tf_op | source)
XLA Modules:
  0.0 144.0 jit_solution(12626673213501004102)
XLA Ops:
  0.6 142.1 %shard_map.110 = (bf16[160,2048]{1,0:T(8,128)(2,1)S(1)}, bf16[8,160]{1,0:T(8,128)(2,1)S(1)}, bf16[1,256,768]{2,1,0:T(8,128)(2,1)S(1)}, bf16[1,256,768]{2,1,0:T(8,128)(2,1)S(1)}, bf16[1,768,256]{2,1,0:T(8,128)(2,1)S(1)}) custom-call(s32[8,160]{1,0:T(8,128)} %bitcast.3, bf16[8,160]{1,0:T(8,128)(2,1)} %bitcast.4, bf16[160,2048]{1,0:T(8,128)(2,1)} %tok_hbm.1, ...), custom_call_target="tpu_custom_call" | custom-call | tf_op jit(solution)/shard_map/pallas_call | solution.py:469
  142.8 1.3 shard_map.111
